TPU v7x, 512 devices: a whole 4x4x16 slice. The times are simulated.
512 devices in a mesh: ctx: 64 (over y, z), tp: 8 (over x, core).
Axes of the slice: x: 4, y: 4, z: 16, core: 2. Of those that a mesh axis runs over, the one named last changes fastest.
Arguments:
- gate_out: bfloat16 [32768, 4096], P('ctx', 'tp'), may hold values from -6 to 6
- gate_in: bfloat16 [32768, 4096], P('ctx', 'tp'), may hold values from -6 to 6
- signal: bfloat16 [32768, 4096], P('ctx', 'tp'), may hold values from -6 to 6
- decay_rates: float32 [16, 4096], P(None, 'tp'), may hold values from 9.765625e-07 to 0.1, as said below
- residues: float32 [16, 4096], P(None, 'tp'), may hold values from -0.6 to 0.6
- skip_gain: float32 [4096], P('tp'), may hold values from -4 to 4
- out_proj: bfloat16 [4096, 4096], P('tp'), may hold values from -0.09375 to 0.09375
- doc_lengths: int32 [32], replicated, may hold values from 1 to 20480, 32768 in all
Outputs:
- layer_out: bfloat16 [32768, 4096], P(('ctx', 'tp'))
Inputs may be any that keep to these rules, and one draw needn't show every extreme that they name: `doc_lengths`: 32 documents laid end to end, lengths summing to 32768. `decay_rates`: positive.
All inputs are finite; a program needn't handle non-finite values.
Results may differ from a plain program's by a relative error of at most 0.017.
Values may be sent and summed in bfloat16 or wider, within the bound.
No kernel may reach another device: no remote copies, remote signals or barrier semaphores. Data moves between devices by JAX's collectives and lax.ppermute only.
A program may use at most 64 MiB of HBM per device.

v0:
```python
import jax
import jax.numpy as jnp
from jax import lax
from jax.sharding import PartitionSpec as P

precise = lax.Precision.HIGHEST


def per_device(gate_out, gate_in, signal, decay_rates, residues, skip_gain, out_proj, doc_lengths):
    length = signal.shape[0]
    channels = signal.shape[1]
    block_len = min(32, length)
    num_blocks = length // block_len
    my_shard = lax.axis_index("ctx")
    shard_begin = my_shard * length
    doc_ends = jnp.cumsum(doc_lengths)
    doc_starts = doc_ends - doc_lengths
    positions = shard_begin + jnp.arange(length, dtype=jnp.int32)
    doc_index = jnp.sum((doc_starts[None, :] <= positions[:, None]).astype(jnp.int32), axis=1)
    opening = jnp.any(doc_starts[None, :] == positions[:, None], axis=1)
    head_start = jnp.max(jnp.where(doc_starts <= shard_begin, doc_starts, 0))
    open_shard = ((doc_index == doc_index[0]) & (head_start < shard_begin)).astype(jnp.float32)
    anchor = head_start // length
    feed_in = gate_in.astype(jnp.float32) * signal.astype(jnp.float32)
    lag_steps = jnp.arange(block_len, dtype=jnp.float32)
    lag_decay = jnp.exp(-lag_steps[None, :, None] * decay_rates[:, None, :])
    filter_taps = jnp.einsum("nkc,nc->kc", lag_decay, residues, precision=precise)
    lag_ids = jnp.arange(block_len, dtype=jnp.int32)
    onehot = (lag_ids[:, None, None] - lag_ids[None, :, None] == lag_ids[None, None, :]).astype(
        jnp.float32
    )
    toeplitz = jnp.einsum("tsk,kc->tsc", onehot, filter_taps, precision=precise)
    enter_decay = jnp.exp(-(lag_steps + 1.0)[None, :, None] * decay_rates[:, None, :])
    leave_decay = jnp.exp(-(block_len - 1.0 - lag_steps)[None, :, None] * decay_rates[:, None, :])
    block_decay = jnp.exp(-block_len * decay_rates)

    def advance(carry_state, inputs):
        block_rows, block_docs, block_marks = inputs
        same_doc = (block_docs[:, None] == block_docs[None, :]).astype(jnp.float32)
        within = jnp.einsum(
            "tsc,sc->tc", toeplitz * same_doc[:, :, None], block_rows, precision=precise
        )
        before = (jnp.cumsum(block_marks.astype(jnp.int32)) == 0).astype(jnp.float32)
        incoming = (
            jnp.einsum("ntc,nc->tc", enter_decay, residues * carry_state, precision=precise)
            * before[:, None]
        )
        tail_mask = (block_docs == block_docs[block_len - 1]).astype(jnp.float32)
        passes = 1.0 - jnp.max(block_marks.astype(jnp.float32))
        added_state = jnp.einsum(
            "nsc,s,sc->nc", leave_decay, tail_mask, block_rows, precision=precise
        )
        return (block_decay * carry_state * passes + added_state, within + incoming)

    zero_state = jnp.zeros((decay_rates.shape[0], channels), jnp.float32)
    end_state, local_out = lax.scan(
        advance,
        zero_state,
        (
            feed_in.reshape(num_blocks, block_len, channels),
            doc_index.reshape(num_blocks, block_len),
            opening.reshape(num_blocks, block_len),
        ),
    )
    local_out = local_out.reshape(length, channels)
    states_part = lax.all_gather(end_state[None], "ctx", axis=0, tiled=True)
    row_count = states_part.shape[0]
    shard_ids = jnp.arange(row_count, dtype=jnp.int32)
    shard_gap = jnp.maximum(my_shard - 1 - shard_ids, 0).astype(jnp.float32)
    in_window = ((shard_ids >= anchor) & (shard_ids < my_shard)).astype(jnp.float32)
    weight = (
        jnp.exp(-(length * shard_gap)[:, None, None] * decay_rates[None, :, :])
        * in_window[:, None, None]
    )
    carried = jnp.sum(weight * states_part, axis=0)
    offsets = jnp.arange(1, length + 1, dtype=jnp.float32)
    decay_out = jnp.exp(-offsets[None, :, None] * decay_rates[:, None, :])
    from_prior = (
        jnp.einsum("ntc,nc->tc", decay_out, residues * carried, precision=precise)
        * open_shard[:, None]
    )
    conv_total = local_out + from_prior + skip_gain[None, :] * feed_in
    hidden = (gate_out.astype(jnp.float32) * conv_total).astype(jnp.bfloat16)
    return lax.psum_scatter(
        jnp.dot(hidden, out_proj, preferred_element_type=jnp.float32).astype(jnp.bfloat16),
        "tp",
        scatter_dimension=0,
        tiled=True,
    )


def solution(mesh):
    return jax.shard_map(
        per_device,
        mesh=mesh,
        in_specs=(
            P("ctx", "tp"),
            P("ctx", "tp"),
            P("ctx", "tp"),
            P(None, "tp"),
            P(None, "tp"),
            P("tp"),
            P("tp", None),
            P(),
        ),
        out_specs=P(("ctx", "tp"), None),
        check_vma=False,
    )
```

profile of v0, /device:TPU:1, one launch (start us, length us, event | category | flops | bytes accessed | tf_op | source)
XLA Modules:
  0.0 296.3 jit_solution(3338242892878419437)
XLA Ops:
  6.5 0.7 copy.14
  7.5 1.3 fusion.11
  9.1 0.9 multiply_exponential_fusion
  10.0 1.0 multiply_reduce_fusion.5
  11.0 1.0 fusion.8
  12.3 79.1 %while.15 = (s32[]{:T(128)}, f32[16,512]{1,0:T(8,128)S(1)}, f32[16,32,512]{2,1,0:T(8,128)}, f32[16,512]{1,0:T(8,128)S(1)}, pred[16,32]{1,0:T(8,128)(4,1)S(1)}, /...) while((s32[]{:T(128)}, f32[16,512]{1,0:T(8,128)S(1)}, ...), condition=%wide.region_6.7_spmd.clone.clone.clone, body=%wide.region_3.6_spmd.clone.clone.clone.sunk | while | flops 3198147 | bytes 3157015 | solution.py:56
  16.5 0.7 bitcast_dynamic-update-slice_fusion.2
  26.4 0.7 bitcast_dynamic-update-slice_fusion.2
  31.4 0.7 bitcast_dynamic-update-slice_fusion.2
  36.3 0.7 bitcast_dynamic-update-slice_fusion.2
  41.2 0.7 bitcast_dynamic-update-slice_fusion.2
  46.2 0.7 bitcast_dynamic-update-slice_fusion.2
  51.1 0.7 bitcast_dynamic-update-slice_fusion.2
  61.0 0.7 bitcast_dynamic-update-slice_fusion.2
  70.9 0.7 bitcast_dynamic-update-slice_fusion.2
  80.8 0.7 bitcast_dynamic-update-slice_fusion.2
  85.8 0.7 bitcast_dynamic-update-slice_fusion.2
  90.7 0.7 bitcast_dynamic-update-slice_fusion.2
  96.0 133.6 %all-gather.3.cloned.1.call-done = f32[1024,512]{1,0:T(8,128)} async-done(((f32[16,512]{1,0:T(8,128)}), f32[1024,512]{1,0:T(8,128)}) %all-gather.3.cloned.1.call-update) | async-done | bytes 2097168 | tf_op jit(solution)/shard_map/all_gather | solution.py:66
  229.6 2.1 multiply_reduce_fusion.4
  231.8 2.8 multiply_reduce_fusion.3
  235.1 1.8 copy-done.10
  236.9 4.3 %convolution_convert_fusion = bf16[512,4096]{1,0:T(8,128)(2,1)} fusion(bf16[512,512]{1,0:T(8,128)(2,1)S(1)} %fusion.7, bf16[512,4096]{1,0:T(8,128)(2,1)S(1)} %copy-done.10), kind=kOutput, calls=%fused_computation.19 | convolution fusion | flops 2149580800 | bytes 8912896 | tf_op jit(solution)/shard_map/dot_general | solution.py:85
  241.2 48.3 %reduce-scatter.2.cloned.1.call-done = bf16[64,4096]{1,0:T(8,128)(2,1)} async-done(((bf16[512,4096]{1,0:T(8,128)(2,1)}), bf16[64,4096]{1,0:T(8,128)(2,1)}) %reduce-scatter.2.cloned.1.call-update) | async-done | bytes 524304 | tf_op jit(solution)/shard_map/reduce_scatter | solution.py:84
  (305 shorter events, 61.7 us)
Async XLA Ops:
  6.5 223.1 %all-gather.3.cloned.1.call-start = ((), (), s32[]{:S(2)}) async-start(), calls=%async_computation.2 | async-start | bytes 2129920 | tf_op jit(solution)/shard_map/all_gather | solution.py:66
  9.1 2.9 copy-start
  9.1 3.0 copy-start.2
  11.0 1.2 copy-start.4
  11.0 1.2 copy-start.8
  91.4 0.6 copy-start.5
  92.0 197.4 %reduce-scatter.2.cloned.1.call-start = ((), (), s32[]{:S(2)}) async-start(), calls=%async_computation.1 | async-start | bytes 4718592 | tf_op jit(solution)/shard_map/reduce_scatter | solution.py:84
  231.7 2.9 copy-start.1
  231.8 2.9 copy-start.3
  231.8 2.9 copy-start.6
  231.8 2.9 copy-start.7
  231.8 2.9 copy-start.9
  234.7 2.2 copy-start.10
Sparse Core Ops, SparseCore 0:
  92.2 137.4 all-gather.2
  241.3 48.0 reduce-scatter.1
where the time goes:
time: 298 us; the launch traced here: 296 us
  waiting for transfers between devices  182 us (61%)
  other arithmetic  64.3 us (22%)
  between operations  16.4 us (6%)
  local copies, waits for them, and re-layouts  16.3 us (5%)
  loops' own time  12 us (4%)
  matrix products  5.35 us (2%)
    all_gather x1, waiting for transfers between devices, per_device(): states_part = lax.all_gather(end_state[None], 'ctx', axis=0, tiled=True)  134 us
    reduce_scatter x1, waiting for transfers between devices, per_device(): lax.psum_scatter(jnp.dot(hidden, out_proj, preferred_element_type=jnp.flo...  48.3 us
    another operation x34, other arithmetic  12.2 us
    another operation x1, loops' own time, per_device(): lax.scan(advance, zero_state, (feed_in.reshape(num_blocks, block_len, cha...  12 us
    dynamic_update_slice x16, other arithmetic, per_device(): lax.scan(advance, zero_state, (feed_in.reshape(num_blocks, block_len, cha...  11.2 us
    reduce_max x16, other arithmetic, advance(): passes = 1.0 - jnp.max(block_marks.astype(jnp.float32))  11.1 us
    slice x16, local copies, waits for them, and re-layouts, advance(): tail_mask = (block_docs == block_docs[block_len - 1]).astype(jnp.float32)  10.6 us
    dot_general x16, other arithmetic, advance(): jnp.einsum('tsc,sc->tc', toeplitz * same_doc[:, :, None], block_rows, pre...  7.12 us
  transfers between devices with their start and end apart: 2, of which 2 were waited for; matrix products, arithmetic and copies ran while one was open for 0% of the time, Pallas kernels for 0%

commit v1 on v0

v1 whole, which is shorter than its diff:
```python
import functools

import jax
import jax.numpy as jnp
from jax import lax
from jax.experimental import pallas as pl
from jax.experimental.pallas import tpu as pltpu
from jax.sharding import PartitionSpec as P

F32 = jnp.float32
BF16 = jnp.bfloat16
Z_AXIS, CORES = 16, 2
SUB = 8
LANES = 128


def smem():
    return pl.BlockSpec(memory_space=pltpu.SMEM)


def vmem():
    return pl.BlockSpec(memory_space=pltpu.VMEM)


def starts_of(lengths_ref):
    at = jnp.int32(0)
    starts = []
    for j in range(lengths_ref.shape[0]):
        starts.append(at)
        at = at + lengths_ref[j]
    return starts


def state_kernel(lengths_ref, gate_ref, signal_ref, rates_ref, feed_ref, enter_ref, send_ref, ends_ref):
    length = gate_ref.shape[0]
    modes = rates_ref.shape[0]
    chunk = length // SUB
    begin = lax.axis_index("ctx") * length
    feed_ref[0] = gate_ref[...].astype(F32) * signal_ref[...].astype(F32)
    chunk_begin = begin + chunk * lax.broadcasted_iota(jnp.int32, (SUB, LANES), 0)
    last = jnp.full((SUB, LANES), -1, jnp.int32)
    for start in starts_of(lengths_ref):
        offset = start - chunk_begin
        last = jnp.where((offset >= 0) & (offset < chunk), jnp.maximum(last, offset), last)
    whole = (last < 0).astype(F32)
    decay = jnp.exp(-rates_ref[...])
    steps = [jnp.broadcast_to(decay[n : n + 1, :], (SUB, LANES)) for n in range(modes)]

    def advance(i, states):
        row = feed_ref[0, pl.ds(i, SUB, stride=chunk), :]
        row = jnp.where(last <= i, row, 0.0)
        return tuple(s * a + row for s, a in zip(states, steps))

    zero = jnp.zeros((SUB, LANES), F32)
    states = lax.fori_loop(0, chunk, advance, (zero,) * modes, unroll=4)
    for n in range(modes):
        ends_ref[SUB * n : SUB * n + SUB, :] = states[n]
    chunk_decay = jnp.exp(-float(chunk) * rates_ref[...])
    carry = jnp.zeros((modes, LANES), F32)
    for s in range(SUB):
        enter_ref[0, pl.ds(s, modes, stride=SUB), :] = carry
        passed = jnp.broadcast_to(whole[s : s + 1, :], (modes, LANES))
        carry = carry * chunk_decay * passed + ends_ref[pl.ds(s, modes, stride=SUB), :]
    rounded = carry.astype(BF16)
    for r in range(send_ref.shape[0]):
        send_ref[r] = rounded


def local_kernel(lengths_ref, feed_ref, enter_ref, rates_ref, residues_ref, skip_ref, out_ref, info_ref, mark_ref):
    length = feed_ref.shape[1]
    modes = rates_ref.shape[0]
    chunk = length // SUB
    place = lax.axis_index("ctx")
    begin = place * length

    @pl.when(pl.program_id(0) == 0)
    def _():
        starts = starts_of(lengths_ref)
        first = jnp.int32(length)
        for start in starts:
            inside = (start >= begin) & (start < begin + length)
            first = jnp.where(inside, jnp.minimum(first, start - begin), first)
        info_ref[0] = first
        for to in range(info_ref.shape[0] - 1):
            target = (to * Z_AXIS + place % Z_AXIS) * length
            head = jnp.int32(0)
            for start in starts:
                head = jnp.where(start <= target, jnp.maximum(head, start), head)
            info_ref[1 + to] = head // length
        mark_ref[...] = jnp.ones(mark_ref.shape, F32)
        for start in starts:

            @pl.when((start >= begin) & (start < begin + length))
            def _(start=start):
                offset = start - begin
                at = lax.rem(offset, chunk)
                rows = lax.broadcasted_iota(jnp.int32, (SUB, LANES), 0)
                mark_ref[at] = jnp.where(rows == offset // chunk, 0.0, mark_ref[at])

    decay = jnp.exp(-rates_ref[...])
    steps = [jnp.broadcast_to(decay[n : n + 1, :], (SUB, LANES)) for n in range(modes)]
    skip = jnp.broadcast_to(skip_ref[...], (SUB, LANES))

    def advance(i, states):
        fed = feed_ref[0, pl.ds(i, SUB, stride=chunk), :]
        kept = mark_ref[i]
        new = tuple(s * (a * kept) + fed for s, a in zip(states, steps))
        total = skip * fed
        for n in range(modes):
            total = total + jnp.broadcast_to(residues_ref[n : n + 1, :], (SUB, LANES)) * new[n]
        out_ref[0, pl.ds(i, SUB, stride=chunk), :] = total
        return new

    init = tuple(enter_ref[0, SUB * n : SUB * n + SUB, :] for n in range(modes))
    lax.fori_loop(0, chunk, advance, init, unroll=2)


def relay_kernel(info_ref, states_ref, rates_ref, out_ref, *, length):
    place = lax.axis_index("ctx")
    line = states_ref.shape[0]
    row = place // line
    at = place % line
    span = float(length) * rates_ref[...]
    decay = jnp.exp(-span)
    states = [states_ref[z].astype(F32) for z in range(line)]
    for to in range(out_ref.shape[0]):
        anchor = info_ref[1 + to]
        stop = jnp.where(to == row, at, jnp.where(to > row, line, 0))
        total = jnp.zeros(rates_ref.shape, F32)
        for z in range(line):
            grown = total * decay + jnp.where(row * line + z >= anchor, states[z], 0.0)
            total = jnp.where(z < stop, grown, total)
        gap = jnp.where(to > row, (to - row - 1) * line + at, 0)
        out_ref[to] = (total * jnp.exp(-gap.astype(F32) * span)).astype(BF16)


def hidden_kernel(info_ref, shares_ref, rates_ref, residues_ref, local_ref, gate_ref, mine_ref, other_ref, prior_ref):
    length = gate_ref.shape[0]
    modes = rates_ref.shape[0]
    chunk = length // SUB
    carried = shares_ref[0].astype(F32)
    for g in range(1, shares_ref.shape[0]):
        carried = carried + shares_ref[g].astype(F32)
    carried = carried * residues_ref[...]
    decay = jnp.exp(-rates_ref[...])
    chunk_begin = chunk * lax.broadcasted_iota(jnp.int32, (SUB, LANES), 0)
    ahead = info_ref[0] - chunk_begin
    ages = chunk_begin.astype(F32)
    steps = [jnp.broadcast_to(decay[n : n + 1, :], (SUB, LANES)) for n in range(modes)]

    def advance(i, states):
        new = tuple(s * a for s, a in zip(states, steps))
        sums = list(new)
        while len(sums) > 1:
            sums = [sums[k] + sums[k + 1] for k in range(0, len(sums), 2)]
        prior_ref[pl.ds(i, SUB, stride=chunk), :] = jnp.where(ahead > i, sums[0], 0.0)
        return new

    init = []
    for n in range(modes):
        rate = jnp.broadcast_to(rates_ref[n : n + 1, :], (SUB, LANES))
        init.append(jnp.exp(-ages * rate) * jnp.broadcast_to(carried[n : n + 1, :], (SUB, LANES)))
    lax.fori_loop(0, chunk, advance, tuple(init), unroll=4)
    core = lax.axis_index("tp") % CORES
    for x in range(SUB // CORES):
        for side, ref in ((core, mine_ref), (1 - core, other_ref)):
            rows = pl.ds(pl.multiple_of((x * CORES + side) * chunk, chunk), chunk)
            mixed = local_ref[0, rows, :] + prior_ref[rows, :]
            ref[x * chunk : (x + 1) * chunk, :] = (gate_ref[rows, :].astype(F32) * mixed).astype(BF16)


def project_kernel(mine_ref, peer_ref, own_ref, far_ref, out_ref):
    total = jnp.dot(mine_ref[...], own_ref[...], preferred_element_type=F32)
    total = total + jnp.dot(peer_ref[...], far_ref[...], preferred_element_type=F32)
    out_ref[...] = total.astype(BF16)


def kept_kernel(mine_ref, peer_ref, own_ref, far_ref, out_ref):
    keep = out_ref.shape[0]
    rows = pl.ds(pl.multiple_of(lax.axis_index("tp") // CORES * keep, keep), keep)
    total = jnp.dot(mine_ref[rows, :], own_ref[...], preferred_element_type=F32)
    out_ref[...] = total + jnp.dot(peer_ref[rows, :], far_ref[...], preferred_element_type=F32)


def total_kernel(pieces_ref, kept_ref, out_ref):
    chip = lax.axis_index("tp") // CORES
    total = kept_ref[...]
    for x in range(pieces_ref.shape[0]):
        total = total + jnp.where(chip == x, 0.0, pieces_ref[x].astype(F32))
    out_ref[...] = total.astype(BF16)


def cost(flops, moved):
    return pl.CostEstimate(flops=int(flops), bytes_accessed=int(moved), transcendentals=0)


def limit(mib=60):
    return pltpu.CompilerParams(vmem_limit_bytes=mib * 1024 * 1024)


def per_device(gate_out, gate_in, signal, decay_rates, residues, skip_gain, out_proj, doc_lengths, *, shards, lanes):
    length, channels = signal.shape
    modes = decay_rates.shape[0]
    width = out_proj.shape[1]
    pairs = [(t, t ^ 1) for t in range(lanes)]
    tiles = channels // LANES
    columns_y = shards // Z_AXIS
    half = length // CORES
    columns = lambda rows: pl.BlockSpec((rows, LANES), lambda g: (0, g))
    stack = lambda rows: pl.BlockSpec((1, rows, LANES), lambda g: (g, 0, 0))
    pages = lambda count: pl.BlockSpec((count, modes, LANES), lambda g: (0, 0, g))

    feed, enter, send = pl.pallas_call(
        state_kernel,
        name="state",
        grid=(tiles,),
        in_specs=[smem(), columns(length), columns(length), columns(modes)],
        out_specs=[stack(length), stack(modes * SUB), pages(Z_AXIS)],
        out_shape=[
            jax.ShapeDtypeStruct((tiles, length, LANES), F32),
            jax.ShapeDtypeStruct((tiles, modes * SUB, LANES), F32),
            jax.ShapeDtypeStruct((Z_AXIS, modes, channels), BF16),
        ],
        scratch_shapes=[pltpu.VMEM((modes * SUB, LANES), F32)],
        compiler_params=limit(),
        cost_estimate=cost(4 * length * channels * modes, 3 * length * channels * 4),
    )(doc_lengths, gate_in, signal, decay_rates)

    send, out_proj = lax.optimization_barrier((send, out_proj))
    far_proj = lax.ppermute(out_proj, "tp", pairs)
    row_groups = [[y * Z_AXIS + z for z in range(Z_AXIS)] for y in range(columns_y)]
    states = lax.all_to_all(send, "ctx", 0, 0, axis_index_groups=row_groups, tiled=True)

    local, info = pl.pallas_call(
        local_kernel,
        name="local",
        grid=(tiles,),
        in_specs=[smem(), stack(length), stack(modes * SUB), columns(modes), columns(modes), columns(1)],
        out_specs=[stack(length), smem()],
        out_shape=[
            jax.ShapeDtypeStruct((tiles, length, LANES), F32),
            jax.ShapeDtypeStruct((1 + columns_y,), jnp.int32),
        ],
        scratch_shapes=[pltpu.VMEM((length // SUB, SUB, LANES), F32)],
        compiler_params=limit(),
        cost_estimate=cost(8 * length * channels * modes, 2 * length * channels * 4),
    )(doc_lengths, feed, enter, decay_rates, residues, skip_gain.reshape(1, channels))

    shares = pl.pallas_call(
        functools.partial(relay_kernel, length=length),
        name="relay",
        in_specs=[smem(), vmem(), vmem()],
        out_specs=vmem(),
        out_shape=jax.ShapeDtypeStruct((columns_y, modes, channels), BF16),
        compiler_params=limit(8),
        cost_estimate=cost(64 * modes * channels * 4, 20 * modes * channels * 2),
    )(info, states, decay_rates)

    column_groups = [[y * Z_AXIS + z for y in range(columns_y)] for z in range(Z_AXIS)]
    shares = lax.all_to_all(shares, "ctx", 0, 0, axis_index_groups=column_groups, tiled=True)

    mine, other = pl.pallas_call(
        hidden_kernel,
        name="hidden",
        grid=(tiles,),
        in_specs=[smem(), pages(columns_y), columns(modes), columns(modes), stack(length), columns(length)],
        out_specs=[columns(half)] * 2,
        out_shape=[jax.ShapeDtypeStruct((half, channels), BF16)] * 2,
        scratch_shapes=[pltpu.VMEM((length, LANES), F32)],
        compiler_params=limit(),
        cost_estimate=cost(3 * length * channels * modes, 2 * length * channels * 4),
    )(info, shares, decay_rates, residues, local, gate_out)

    peer = lax.ppermute(other, "tp", pairs)
    chips = lanes // CORES
    chip_groups = [[x * CORES + c for x in range(chips)] for c in range(CORES)]
    keep = half // chips
    tile = min(1024, width)
    weights = pl.BlockSpec((channels, tile), lambda j: (0, j))
    rows = pl.BlockSpec((half, channels), lambda j: (0, 0))
    sent = pl.pallas_call(
        project_kernel,
        name="project",
        grid=(width // tile,),
        in_specs=[rows, rows, weights, weights],
        out_specs=pl.BlockSpec((half, tile), lambda j: (0, j)),
        out_shape=jax.ShapeDtypeStruct((half, width), BF16),
        compiler_params=limit(),
        cost_estimate=cost(4 * half * channels * width, 4 * channels * width),
    )(mine, peer, out_proj, far_proj)
    pieces = lax.all_to_all(sent, "tp", 0, 0, axis_index_groups=chip_groups, tiled=True)

    kept = pl.pallas_call(
        kept_kernel,
        name="kept",
        grid=(width // tile,),
        in_specs=[rows, rows, weights, weights],
        out_specs=pl.BlockSpec((keep, tile), lambda j: (0, j)),
        out_shape=jax.ShapeDtypeStruct((keep, width), F32),
        compiler_params=limit(),
        cost_estimate=cost(4 * half * channels * width, 4 * channels * width),
    )(mine, peer, out_proj, far_proj)

    return pl.pallas_call(
        total_kernel,
        name="total",
        grid=(width // tile,),
        in_specs=[
            pl.BlockSpec((chips, keep, tile), lambda j: (0, 0, j)),
            pl.BlockSpec((keep, tile), lambda j: (0, j)),
        ],
        out_specs=pl.BlockSpec((keep, tile), lambda j: (0, j)),
        out_shape=jax.ShapeDtypeStruct((keep, width), BF16),
        compiler_params=limit(16),
        cost_estimate=cost(chips * keep * width, 2 * chips * keep * width),
    )(pieces.reshape(chips, keep, width), kept)


def solution(mesh):
    body = functools.partial(per_device, shards=mesh.shape["ctx"], lanes=mesh.shape["tp"])
    return jax.shard_map(
        body,
        mesh=mesh,
        in_specs=(
            P("ctx", "tp"),
            P("ctx", "tp"),
            P("ctx", "tp"),
            P(None, "tp"),
            P(None, "tp"),
            P("tp"),
            P("tp", None),
            P(),
        ),
        out_specs=P(("ctx", "tp"), None),
        check_vma=False,
    )
```

time: 298 us -> 103 us (0.35)
  waiting for transfers between devices: 182 us -> 27.8 us
  other arithmetic: 64.3 us -> 0 us
  Pallas kernels: 0 us -> 32.1 us
  starting transfers between devices: 0.04 us -> 30.4 us
  between operations: 16.4 us -> 0.04 us
  local copies, waits for them, and re-layouts: 16.3 us -> 3.32 us
  loops' own time: 12 us -> 0 us
  blocking collectives: 0 us -> 8.57 us
  matrix products: 5.35 us -> 0 us
    all_gather x1 -> x0, waiting for transfers between devices: 134 us -> none  [per_device(): states_part = lax.all_gather(end_state[None], 'ctx', axis=0, tiled=True)]
    reduce_scatter x1 -> x0, waiting for transfers between devices: 48.3 us -> none  [per_device(): lax.psum_scatter(jnp.dot(hidden, out_proj, preferred_element_type=jnp.flo...]
    pallas_call x0 -> x7, Pallas kernels: none -> 32.1 us  [the longest x1 7.82 us: per_device(): pl.pallas_call(local_kernel, name='local', grid=(tiles,), in_specs=[smem(...]
    all_to_all x0 -> x2, waiting for transfers between devices: none -> 26.5 us  [the longest x1 19.9 us: per_device(): lax.all_to_all(sent, 'tp', 0, 0, axis_index_groups=chip_groups, tiled=True)]
    dot_general x50 -> x0, other arithmetic: 19.6 us -> none  [the longest x16 7.12 us: advance(): jnp.einsum('tsc,sc->tc', toeplitz * same_doc[:, :, None], block_rows, pre...]
    ppermute x0 -> x2, starting transfers between devices: none -> 16.8 us  [the longest x1 8.78 us: per_device(): far_proj = lax.ppermute(out_proj, 'tp', pairs)]
    all_to_all x0 -> x2, starting transfers between devices: none -> 13.6 us  [the longest x1 9.55 us: per_device(): lax.all_to_all(send, 'ctx', 0, 0, axis_index_groups=row_groups, tiled=True)]
    reduce_max x17 -> x0, other arithmetic: 12.3 us -> none  [the longest x16 11.1 us: advance(): passes = 1.0 - jnp.max(block_marks.astype(jnp.float32))]
  transfers between devices with their start and end apart: 2 -> 4, of which waited for: 2 -> 3; matrix products, arithmetic and copies ran while one was open for 0% -> 0% of each run, Pallas kernels for 0% -> 19%
where the time goes in v1:
time: 103 us; the launch traced here: 102 us
  Pallas kernels  32.1 us (31%)
  starting transfers between devices  30.4 us (30%)
  waiting for transfers between devices  27.8 us (27%)
  blocking collectives  8.57 us (8%)
  local copies, waits for them, and re-layouts  3.32 us (3%)
    all_to_all x1, waiting for transfers between devices, per_device(): lax.all_to_all(sent, 'tp', 0, 0, axis_index_groups=chip_groups, tiled=True)  19.9 us
    all_to_all x1, starting transfers between devices, per_device(): lax.all_to_all(send, 'ctx', 0, 0, axis_index_groups=row_groups, tiled=True)  9.55 us
    ppermute x1, starting transfers between devices, per_device(): far_proj = lax.ppermute(out_proj, 'tp', pairs)  8.78 us
    all_to_all x1, blocking collectives, per_device(): lax.all_to_all(shares, 'ctx', 0, 0, axis_index_groups=column_groups, tile...  8.57 us
    ppermute x1, starting transfers between devices, per_device(): peer = lax.ppermute(other, 'tp', pairs)  8.06 us
    pallas_call x1, Pallas kernels, per_device(): pl.pallas_call(local_kernel, name='local', grid=(tiles,), in_specs=[smem(...  7.82 us
    all_to_all x1, waiting for transfers between devices, per_device(): lax.all_to_all(send, 'ctx', 0, 0, axis_index_groups=row_groups, tiled=True)  6.62 us
    pallas_call x1, Pallas kernels, per_device(): pl.pallas_call(project_kernel, name='project', grid=(width // tile,), in_...  6.58 us
  transfers between devices with their start and end apart: 4, of which 3 were waited for; matrix products, arithmetic and copies ran while one was open for 0% of the time, Pallas kernels for 19%

profile of v1, /device:TPU:1, one launch (start us, length us, event | category | flops | bytes accessed | tf_op | source)
XLA Modules:
  0.0 102.3 jit_solution(4835298647571999538)
XLA Ops:
  0.0 4.6 %state.1 = (f32[4,512,128]{2,1,0:T(8,128)}, f32[4,128,128]{2,1,0:T(8,128)}, bf16[16,16,512]{2,1,0:T(8,128)(2,1)}) custom-call(s32[32]{0:T(128)} %lengths_ref.3, bf16[512,512]{1,0:T(8,128)(2,1)} %gate_ref.2, bf16[512,512]{1,0:T(8,128)(2,1)} %signal_ref.1, f32[16,512]{1,0:T(8,128)} %rates_ref.7), custom_call_target="tpu_custom_call" | custom-call | flops 16777216 | bytes 3145728 | tf_op jit(solution)/shard_map/state/pallas_call | solution.py:213
  4.6 8.8 %collective-permute-start.1 = (bf16[512,4096]{1,0:T(8,128)(2,1)}, bf16[512,4096]{1,0:T(8,128)(2,1)}, u32[]{:S(2)}, u32[]{:S(2)}) collective-permute-start(bf16[512,4096]{1,0:T(8,128)(2,1)} %own_ref.1), channel_id=1, source_target_pairs={{0,1},{1,0},{2,3},{3,2},{4,5},{5,4},{6,7},{7,6},{8,9},{9,8},{10,11... | collective-permute-start | bytes 12582920 | tf_op jit(solution)/shard_map/ppermute | solution.py:230
  13.4 9.6 %all-to-all-start = ((bf16[16,16,512]{2,1,0:T(8,128)(2,1)}), bf16[16,16,512]{2,1,0:T(8,128)(2,1)S(1)}, u32[]{:S(2)}, u32[]{:S(2)}) async-start(bf16[16,16,512]{2,1,0:T(8,128)(2,1)} %get-tuple-element.18), calls=%async_computation | async-start | bytes 524288 | tf_op jit(solution)/shard_map/all_to_all | solution.py:232
  23.0 7.8 %local.1 = (f32[4,512,128]{2,1,0:T(8,128)}, s32[5]{0:T(128)}) custom-call(s32[32]{0:T(128)} %lengths_ref.3, f32[4,512,128]{2,1,0:T(8,128)} %get-tuple-element.14.feed_ref, f32[4,128,128]{2,1,0:T(8,128)} %get-tuple-element.15.enter_ref, f32[16,512]{1,0:T(8,128)} %rates_ref.7, f32[16,512]{1,0:T(8,128)} %residues_ref.3, f32[1,512]{1,0:T(1,128)} %bitcast.3), custom_call_target="tpu_custom_call" | custom-call | flops 33554432 | bytes 2097152 | tf_op jit(solution)/shard_map/local/pallas_call | solution.py:234
  30.8 6.6 %all-to-all-done.states_ref = bf16[16,16,512]{2,1,0:T(8,128)(2,1)S(1)} async-done(((bf16[16,16,512]{2,1,0:T(8,128)(2,1)}), bf16[16,16,512]{2,1,0:T(8,128)(2,1)S(1)}, u32[]{:S(2)}, u32[]{:S(2)}) %all-to-all-start) | async-done | bytes 262176 | tf_op jit(solution)/shard_map/all_to_all | solution.py:232
  37.4 0.0 copy-start.1
  37.4 0.8 copy-done.1
  38.2 0.0 copy-start.2
  38.2 0.7 copy-done.2
  38.9 1.0 relay.1
  39.8 8.6 %all_to_all.19.shares_ref = bf16[4,16,512]{2,1,0:T(8,128)(2,1)} all-to-all(bf16[4,16,512]{2,1,0:T(8,128)(2,1)S(1)} %relay.1), channel_id=1, replica_groups={{0,128,256,384},{8,136,264,392},{16,144,272,400},{24,152,280,408},{32,1..., dimensions={0} | all-to-all | bytes 131072 | tf_op jit(solution)/shard_map/all_to_all | solution.py:260
  48.4 4.3 %hidden.1 = (bf16[256,512]{1,0:T(8,128)(2,1)}, bf16[256,512]{1,0:T(8,128)(2,1)}) custom-call(s32[5]{0:T(128)} %get-tuple-element.16.info_ref, bf16[4,16,512]{2,1,0:T(8,128)(2,1)} %all_to_all.19.shares_ref, f32[16,512]{1,0:T(8,128)} %rates_ref.7, f32[16,512]{1,0:T(8,128)} %residues_ref.3, f32[4,512,128]{2,1,0:T(8,128)} %get-tuple-element.19.local_ref, ...), custom_call_target="tpu_custom_call" | custom-call | flops 12582912 | bytes 2097152 | tf_op jit(solution)/shard_map/hidden/pallas_call | solution.py:262
  52.7 8.1 %collective-permute-start = (bf16[256,512]{1,0:T(8,128)(2,1)}, bf16[256,512]{1,0:T(8,128)(2,1)S(1)}, u32[]{:S(2)}, u32[]{:S(2)}) collective-permute-start(bf16[256,512]{1,0:T(8,128)(2,1)} %get-tuple-element.21), channel_id=1, source_target_pairs={{0,1},{1,0},{2,3},{3,2},{4,5},{5,4},{6,7},{7,6},{8,9},{9,8},{10,11... | collective-permute-start | bytes 786440 | tf_op jit(solution)/shard_map/ppermute | solution.py:274
  60.8 1.4 %collective-permute-done.peer_ref = bf16[256,512]{1,0:T(8,128)(2,1)S(1)} collective-permute-done((bf16[256,512]{1,0:T(8,128)(2,1)}, bf16[256,512]{1,0:T(8,128)(2,1)S(1)}, u32[]{:S(2)}, u32[]{:S(2)}) %collective-permute-start) | collective-permute-done | bytes 262176 | tf_op jit(solution)/shard_map/ppermute | solution.py:274
  62.1 0.0 copy-start.3
  62.1 0.0 collective-permute-done.1.far_ref
  62.1 0.7 copy-done.3
  62.8 6.6 %project.1 = bf16[256,4096]{1,0:T(8,128)(2,1)} custom-call(bf16[256,512]{1,0:T(8,128)(2,1)} %get-tuple-element.20.mine_ref, bf16[256,512]{1,0:T(8,128)(2,1)} %copy-done.3, bf16[512,4096]{1,0:T(8,128)(2,1)} %own_ref.1, bf16[512,4096]{1,0:T(8,128)(2,1)} %collective-permute-done.1.far_ref), custom_call_target="tpu_custom_call" | custom-call | flops 2147483648 | bytes 8388608 | tf_op jit(solution)/shard_map/project/pallas_call | solution.py:281
  69.4 4.0 %all-to-all-start.2 = ((bf16[4,64,4096]{2,1,0:T(8,128)(2,1)}), bf16[4,64,4096]{2,1,0:T(8,128)(2,1)S(1)}, u32[]{:S(2)}, u32[]{:S(2)}) async-start(bf16[4,64,4096]{2,1,0:T(8,128)(2,1)} %bitcast.2), calls=%async_computation.2 | async-start | bytes 4194304 | tf_op jit(solution)/shard_map/all_to_all | solution.py:291
  73.4 5.9 %kept.1.kept_ref = f32[64,4096]{1,0:T(8,128)} custom-call(bf16[256,512]{1,0:T(8,128)(2,1)} %get-tuple-element.20.mine_ref, bf16[256,512]{1,0:T(8,128)(2,1)} %copy-done.3, bf16[512,4096]{1,0:T(8,128)(2,1)} %own_ref.1, bf16[512,4096]{1,0:T(8,128)(2,1)} %collective-permute-done.1.far_ref), custom_call_target="tpu_custom_call" | custom-call | flops 2147483648 | bytes 8388608 | tf_op jit(solution)/shard_map/kept/pallas_call | solution.py:293
  79.3 19.9 %all-to-all-done.2.pieces_ref = bf16[4,64,4096]{2,1,0:T(8,128)(2,1)S(1)} async-done(((bf16[4,64,4096]{2,1,0:T(8,128)(2,1)}), bf16[4,64,4096]{2,1,0:T(8,128)(2,1)S(1)}, u32[]{:S(2)}, u32[]{:S(2)}) %all-to-all-start.2) | async-done | bytes 2097184 | tf_op jit(solution)/shard_map/all_to_all | solution.py:291
  99.2 0.0 copy-start
  99.2 1.2 %copy-done = f32[64,4096]{1,0:T(8,128)S(1)} copy-done((f32[64,4096]{1,0:T(8,128)S(1)}, f32[64,4096]{1,0:T(8,128)}, u32[]{:S(2)}) %copy-start) | copy-done | bytes 1048600
  100.4 1.9 %total.1 = bf16[64,4096]{1,0:T(8,128)(2,1)} custom-call(bf16[4,64,4096]{2,1,0:T(8,128)(2,1)S(1)} %all-to-all-done.2.pieces_ref, f32[64,4096]{1,0:T(8,128)S(1)} %copy-done), custom_call_target="tpu_custom_call" | custom-call | flops 1048576 | bytes 2097152 | tf_op jit(solution)/shard_map/total/pallas_call | solution.py:304
Async XLA Ops:
  4.6 57.5 %collective-permute-start.1 = (bf16[512,4096]{1,0:T(8,128)(2,1)}, bf16[512,4096]{1,0:T(8,128)(2,1)}, u32[]{:S(2)}, u32[]{:S(2)}) collective-permute-start(bf16[512,4096]{1,0:T(8,128)(2,1)} %own_ref.1), channel_id=1, source_target_pairs={{0,1},{1,0},{2,3},{3,2},{4,5},{5,4},{6,7},{7,6},{8,9},{9,8},{10,11... | collective-permute-start | bytes 12582920 | tf_op jit(solution)/shard_map/ppermute | solution.py:230
  13.4 24.0 %all-to-all-start = ((bf16[16,16,512]{2,1,0:T(8,128)(2,1)}), bf16[16,16,512]{2,1,0:T(8,128)(2,1)S(1)}, u32[]{:S(2)}, u32[]{:S(2)}) async-start(bf16[16,16,512]{2,1,0:T(8,128)(2,1)} %get-tuple-element.18), calls=%async_computation | async-start | bytes 524288 | tf_op jit(solution)/shard_map/all_to_all | solution.py:232
  37.4 0.8 copy-start.1
  38.2 0.7 copy-start.2
  52.7 9.4 %collective-permute-start = (bf16[256,512]{1,0:T(8,128)(2,1)}, bf16[256,512]{1,0:T(8,128)(2,1)S(1)}, u32[]{:S(2)}, u32[]{:S(2)}) collective-permute-start(bf16[256,512]{1,0:T(8,128)(2,1)} %get-tuple-element.21), channel_id=1, source_target_pairs={{0,1},{1,0},{2,3},{3,2},{4,5},{5,4},{6,7},{7,6},{8,9},{9,8},{10,11... | collective-permute-start | bytes 786440 | tf_op jit(solution)/shard_map/ppermute | solution.py:274
  62.1 0.7 copy-start.3
  69.4 29.8 %all-to-all-start.2 = ((bf16[4,64,4096]{2,1,0:T(8,128)(2,1)}), bf16[4,64,4096]{2,1,0:T(8,128)(2,1)S(1)}, u32[]{:S(2)}, u32[]{:S(2)}) async-start(bf16[4,64,4096]{2,1,0:T(8,128)(2,1)} %bitcast.2), calls=%async_computation.2 | async-start | bytes 4194304 | tf_op jit(solution)/shard_map/all_to_all | solution.py:291
  99.2 1.2 %copy-start = (f32[64,4096]{1,0:T(8,128)S(1)}, f32[64,4096]{1,0:T(8,128)}, u32[]{:S(2)}) copy-start(f32[64,4096]{1,0:T(8,128)} %kept.1.kept_ref) | copy-start | bytes 3145732

commit v2 on v1

--- a/solution.py
+++ b/solution.py
@@ -134,8 +134,23 @@
         out_ref[to] = (total * jnp.exp(-gap.astype(F32) * span)).astype(BF16)
 
 
-def hidden_kernel(info_ref, shares_ref, rates_ref, residues_ref, local_ref, gate_ref, mine_ref, other_ref, prior_ref):
+def hidden_kernel(
+    info_ref, shares_ref, rates_ref, residues_ref, local_ref, gate_ref, proj_ref,
+    mine_ref, other_ref, weights_ref, prior_ref, sems,
+):
     length = gate_ref.shape[0]
+    count = sems.shape[0]
+    depth = proj_ref.shape[0] // count
+    copies = [
+        pltpu.make_async_copy(proj_ref.at[pl.ds(i * depth, depth)], weights_ref.at[pl.ds(i * depth, depth)], sems.at[i])
+        for i in range(count)
+    ]
+
+    @pl.when(pl.program_id(0) == 0)
+    def _():
+        for copy in copies:
+            copy.start()
+
     modes = rates_ref.shape[0]
     chunk = length // SUB
     carried = shares_ref[0].astype(F32)
@@ -168,25 +183,45 @@
             mixed = local_ref[0, rows, :] + prior_ref[rows, :]
             ref[x * chunk : (x + 1) * chunk, :] = (gate_ref[rows, :].astype(F32) * mixed).astype(BF16)
 
-
-def project_kernel(mine_ref, peer_ref, own_ref, far_ref, out_ref):
-    total = jnp.dot(mine_ref[...], own_ref[...], preferred_element_type=F32)
-    total = total + jnp.dot(peer_ref[...], far_ref[...], preferred_element_type=F32)
-    out_ref[...] = total.astype(BF16)
-
-
-def kept_kernel(mine_ref, peer_ref, own_ref, far_ref, out_ref):
-    keep = out_ref.shape[0]
+    @pl.when(pl.program_id(0) == pl.num_programs(0) - 1)
+    def _():
+        for copy in copies:
+            copy.wait()
+
+
+def joined(mine, peer, weights_ref, cols):
+    core = lax.axis_index("tp") % CORES
+    depth = mine.shape[1]
+    own = weights_ref[pl.ds(pl.multiple_of(core * depth, depth), depth), cols]
+    far = weights_ref[pl.ds(pl.multiple_of((1 - core) * depth, depth), depth), cols]
+    total = jnp.dot(mine, own, preferred_element_type=F32)
+    return total + jnp.dot(peer, far, preferred_element_type=F32)
+
+
+def project_kernel(mine_ref, peer_ref, weights_ref, out_ref, kept_ref, sums_ref, slots_ref, sems):
+    count, _, tile = slots_ref.shape
+    keep = kept_ref.shape[0]
     rows = pl.ds(pl.multiple_of(lax.axis_index("tp") // CORES * keep, keep), keep)
-    total = jnp.dot(mine_ref[rows, :], own_ref[...], preferred_element_type=F32)
-    out_ref[...] = total + jnp.dot(peer_ref[rows, :], far_ref[...], preferred_element_type=F32)
+    copies = []
+    for j in range(count):
+        cols = pl.ds(j * tile, tile)
+        sums = sums_ref.at[j % 2]
+        sums[...] = joined(mine_ref[...], peer_ref[...], weights_ref, cols)
+        slots_ref[j] = sums[...].astype(BF16)
+        kept_ref[:, cols] = sums[rows, :]
+        copies.append(pltpu.make_async_copy(slots_ref.at[j], out_ref.at[:, cols], sems.at[j]))
+        copies[j].start()
+    for copy in copies:
+        copy.wait()
 
 
 def total_kernel(pieces_ref, kept_ref, out_ref):
     chip = lax.axis_index("tp") // CORES
-    total = kept_ref[...]
+    tile = out_ref.shape[1]
+    cols = pl.ds(pl.multiple_of(pl.program_id(0) * tile, tile), tile)
+    total = kept_ref[:, cols]
     for x in range(pieces_ref.shape[0]):
-        total = total + jnp.where(chip == x, 0.0, pieces_ref[x].astype(F32))
+        total = total + jnp.where(chip == x, 0.0, pieces_ref[x, :, cols].astype(F32))
     out_ref[...] = total.astype(BF16)
 
 
@@ -194,7 +229,7 @@
     return pl.CostEstimate(flops=int(flops), bytes_accessed=int(moved), transcendentals=0)
 
 
-def limit(mib=60):
+def limit(mib=32):
     return pltpu.CompilerParams(vmem_limit_bytes=mib * 1024 * 1024)
 
 
@@ -203,6 +238,11 @@
     modes = decay_rates.shape[0]
     width = out_proj.shape[1]
     pairs = [(t, t ^ 1) for t in range(lanes)]
+    chip_pairs = [[t, t + 1] for t in range(0, lanes, CORES)]
+    chip_proj = lax.all_gather(out_proj, "tp", axis_index_groups=chip_pairs, tiled=True)
+    gate_out, gate_in, signal, decay_rates, residues, chip_proj = (
+        pltpu.with_memory_space_constraint(v, pltpu.HBM) for v in (gate_out, gate_in, signal, decay_rates, residues, chip_proj)
+    )
     tiles = channels // LANES
     columns_y = shards // Z_AXIS
     half = length // CORES
@@ -226,8 +266,6 @@
         cost_estimate=cost(4 * length * channels * modes, 3 * length * channels * 4),
     )(doc_lengths, gate_in, signal, decay_rates)
 
-    send, out_proj = lax.optimization_barrier((send, out_proj))
-    far_proj = lax.ppermute(out_proj, "tp", pairs)
     row_groups = [[y * Z_AXIS + z for z in range(Z_AXIS)] for y in range(columns_y)]
     states = lax.all_to_all(send, "ctx", 0, 0, axis_index_groups=row_groups, tiled=True)
 
@@ -259,56 +297,47 @@
     column_groups = [[y * Z_AXIS + z for y in range(columns_y)] for z in range(Z_AXIS)]
     shares = lax.all_to_all(shares, "ctx", 0, 0, axis_index_groups=column_groups, tiled=True)
 
-    mine, other = pl.pallas_call(
+    mine, other, weights = pl.pallas_call(
         hidden_kernel,
         name="hidden",
         grid=(tiles,),
-        in_specs=[smem(), pages(columns_y), columns(modes), columns(modes), stack(length), columns(length)],
-        out_specs=[columns(half)] * 2,
-        out_shape=[jax.ShapeDtypeStruct((half, channels), BF16)] * 2,
-        scratch_shapes=[pltpu.VMEM((length, LANES), F32)],
+        in_specs=[smem(), pages(columns_y), columns(modes), columns(modes), stack(length), columns(length),
+                  pl.BlockSpec(memory_space=pl.ANY)],
+        out_specs=[columns(half), columns(half), vmem()],
+        out_shape=[jax.ShapeDtypeStruct((half, channels), BF16)] * 2
+        + [jax.ShapeDtypeStruct((CORES * channels, width), BF16)],
+        scratch_shapes=[pltpu.VMEM((length, LANES), F32), pltpu.SemaphoreType.DMA((4,))],
         compiler_params=limit(),
         cost_estimate=cost(3 * length * channels * modes, 2 * length * channels * 4),
-    )(info, shares, decay_rates, residues, local, gate_out)
+    )(info, shares, decay_rates, residues, local, gate_out, chip_proj)
 
     peer = lax.ppermute(other, "tp", pairs)
     chips = lanes // CORES
     chip_groups = [[x * CORES + c for x in range(chips)] for c in range(CORES)]
     keep = half // chips
-    tile = min(1024, width)
-    weights = pl.BlockSpec((channels, tile), lambda j: (0, j))
-    rows = pl.BlockSpec((half, channels), lambda j: (0, 0))
-    sent = pl.pallas_call(
+    tile = min(512, width)
+    sent, kept = pl.pallas_call(
         project_kernel,
         name="project",
-        grid=(width // tile,),
-        in_specs=[rows, rows, weights, weights],
-        out_specs=pl.BlockSpec((half, tile), lambda j: (0, j)),
-        out_shape=jax.ShapeDtypeStruct((half, width), BF16),
-        compiler_params=limit(),
+        in_specs=[vmem(), vmem(), vmem()],
+        out_specs=[pl.BlockSpec(memory_space=pl.ANY), vmem()],
+        out_shape=[jax.ShapeDtypeStruct((half, width), BF16), jax.ShapeDtypeStruct((keep, width), F32)],
+        scratch_shapes=[
+            pltpu.VMEM((2, half, tile), F32),
+            pltpu.VMEM((width // tile, half, tile), BF16),
+            pltpu.SemaphoreType.DMA((width // tile,)),
+        ],
+        compiler_params=limit(16),
         cost_estimate=cost(4 * half * channels * width, 4 * channels * width),
-    )(mine, peer, out_proj, far_proj)
+    )(mine, peer, weights)
     pieces = lax.all_to_all(sent, "tp", 0, 0, axis_index_groups=chip_groups, tiled=True)
 
-    kept = pl.pallas_call(
-        kept_kernel,
-        name="kept",
-        grid=(width // tile,),
-        in_specs=[rows, rows, weights, weights],
-        out_specs=pl.BlockSpec((keep, tile), lambda j: (0, j)),
-        out_shape=jax.ShapeDtypeStruct((keep, width), F32),
-        compiler_params=limit(),
-        cost_estimate=cost(4 * half * channels * width, 4 * channels * width),
-    )(mine, peer, out_proj, far_proj)
-
+    tile = min(2048, width)
     return pl.pallas_call(
         total_kernel,
         name="total",
         grid=(width // tile,),
-        in_specs=[
-            pl.BlockSpec((chips, keep, tile), lambda j: (0, 0, j)),
-            pl.BlockSpec((keep, tile), lambda j: (0, j)),
-        ],
+        in_specs=[vmem(), vmem()],
         out_specs=pl.BlockSpec((keep, tile), lambda j: (0, j)),
         out_shape=jax.ShapeDtypeStruct((keep, width), BF16),
         compiler_params=limit(16),

time: 103 us -> 108 us (1.049)
  blocking collectives: 8.57 us -> 37.7 us
  waiting for transfers between devices: 27.8 us -> 7.58 us
  between operations: 0.04 us -> 13.5 us
  Pallas kernels: 32.1 us -> 23.6 us
  starting transfers between devices: 30.4 us -> 25.3 us
  local copies, waits for them, and re-layouts: 3.32 us -> 0.01 us
    all_to_all x0 -> x1, blocking collectives: none -> 29.3 us  [per_device(): lax.all_to_all(sent, 'tp', 0, 0, axis_index_groups=chip_groups, tiled=True)]
    all_to_all x1 -> x0, waiting for transfers between devices: 19.9 us -> none  [per_device(): lax.all_to_all(sent, 'tp', 0, 0, axis_index_groups=chip_groups, tiled=True)]
    ppermute x1 -> x0, starting transfers between devices: 8.78 us -> none  [per_device(): far_proj = lax.ppermute(out_proj, 'tp', pairs)]
    pallas_call x2 -> x1, Pallas kernels: 12.5 us -> 3.83 us  [per_device(): pl.pallas_call(project_kernel, name='project', in_specs=[vmem(), vmem(),...]
    all_to_all x1, starting transfers between devices: 9.55 us -> 15.7 us  [per_device(): lax.all_to_all(send, 'ctx', 0, 0, axis_index_groups=row_groups, tiled=True)]
    all_to_all x1 -> x0, starting transfers between devices: 4.01 us -> none  [per_device(): lax.all_to_all(sent, 'tp', 0, 0, axis_index_groups=chip_groups, tiled=True)]
    unnamed x8 -> x4, local copies, waits for them, and re-layouts: 3.32 us -> 0.01 us
    ppermute x1, starting transfers between devices: 8.06 us -> 9.52 us  [per_device(): peer = lax.ppermute(other, 'tp', pairs)]
  transfers between devices with their start and end apart: 4 -> 3, of which waited for: 3 -> 2; matrix products, arithmetic and copies ran while one was open for 0% -> 0% of each run, Pallas kernels for 19% -> 12%
where the time goes in v2:
time: 108 us
  blocking collectives  37.7 us (35%)
  starting transfers between devices  25.3 us (23%)
  Pallas kernels  23.6 us (22%)
  between operations  13.5 us (12%)
  waiting for transfers between devices  7.58 us (7%)
    all_to_all x1, blocking collectives, per_device(): lax.all_to_all(sent, 'tp', 0, 0, axis_index_groups=chip_groups, tiled=True)  29.3 us
    all_to_all x1, starting transfers between devices, per_device(): lax.all_to_all(send, 'ctx', 0, 0, axis_index_groups=row_groups, tiled=True)  15.7 us
    ppermute x1, starting transfers between devices, per_device(): peer = lax.ppermute(other, 'tp', pairs)  9.52 us
    all_to_all x1, blocking collectives, per_device(): lax.all_to_all(shares, 'ctx', 0, 0, axis_index_groups=column_groups, tile...  8.46 us
    pallas_call x1, Pallas kernels, per_device(): pl.pallas_call(local_kernel, name='local', grid=(tiles,), in_specs=[smem(...  7.39 us
    all_to_all x1, waiting for transfers between devices, per_device(): lax.all_to_all(send, 'ctx', 0, 0, axis_index_groups=row_groups, tiled=True)  5.73 us
    pallas_call x1, Pallas kernels, per_device(): pl.pallas_call(hidden_kernel, name='hidden', grid=(tiles,), in_specs=[sme...  5.5 us
    pallas_call x1, Pallas kernels, per_device(): pl.pallas_call(state_kernel, name='state', grid=(tiles,), in_specs=[smem(...  4.5 us
  transfers between devices with their start and end apart: 3, of which 2 were waited for; matrix products, arithmetic and copies ran while one was open for 0% of the time, Pallas kernels for 12%

profile of v2, /device:TPU:1, one launch (start us, length us, event | category | flops | bytes accessed | tf_op | source)
XLA Modules:
  0.0 107.6 jit_solution(2280431357061825510)
XLA Ops:
  6.5 0.0 copy-start
  6.5 0.0 copy-start.1
  6.5 0.0 all-gather.2.cloned.1.call-start
  6.5 0.7 all-gather.2.cloned.1.call-update
  7.3 0.0 copy-done
  7.3 4.5 %state.1 = (f32[4,512,128]{2,1,0:T(8,128)S(1)}, f32[4,128,128]{2,1,0:T(8,128)S(1)}, bf16[16,16,512]{2,1,0:T(8,128)(2,1)}) custom-call(s32[32]{0:T(128)S(1)} %copy-done, bf16[512,512]{1,0:T(8,128)(2,1)} %gate_ref.2, bf16[512,512]{1,0:T(8,128)(2,1)} %signal_ref.1, f32[16,512]{1,0:T(8,128)} %rates_ref.7), custom_call_target="tpu_custom_call" | custom-call | flops 16777216 | bytes 3145728 | tf_op jit(solution)/shard_map/state/pallas_call | solution.py:253
  11.8 15.7 %all-to-all-start = ((bf16[16,16,512]{2,1,0:T(8,128)(2,1)}), bf16[16,16,512]{2,1,0:T(8,128)(2,1)S(1)}, u32[]{:S(2)}, u32[]{:S(2)}) async-start(bf16[16,16,512]{2,1,0:T(8,128)(2,1)} %get-tuple-element.18), calls=%async_computation | async-start | bytes 524288 | tf_op jit(solution)/shard_map/all_to_all | solution.py:270
  27.5 0.0 copy-done.1
  27.5 7.4 %local.1 = (f32[4,512,128]{2,1,0:T(8,128)S(1)}, s32[5]{0:T(128)S(1)}) custom-call(s32[32]{0:T(128)S(1)} %copy-done, f32[4,512,128]{2,1,0:T(8,128)S(1)} %get-tuple-element.15.feed_ref, f32[4,128,128]{2,1,0:T(8,128)S(1)} %get-tuple-element.16.enter_ref, f32[16,512]{1,0:T(8,128)} %rates_ref.7, f32[16,512]{1,0:T(8,128)} %residues_ref.3, f32[1,512]{1,0:T(1,128)S(1)} %bitcast.3), custom_call_target="tpu_custom_call" | custom-call | flops 33554432 | bytes 2097152 | tf_op jit(solution)/shard_map/local/pallas_call | solution.py:272
  34.9 5.7 %all-to-all-done.states_ref = bf16[16,16,512]{2,1,0:T(8,128)(2,1)S(1)} async-done(((bf16[16,16,512]{2,1,0:T(8,128)(2,1)}), bf16[16,16,512]{2,1,0:T(8,128)(2,1)S(1)}, u32[]{:S(2)}, u32[]{:S(2)}) %all-to-all-start) | async-done | bytes 262176 | tf_op jit(solution)/shard_map/all_to_all | solution.py:270
  40.7 1.2 %relay.1 = bf16[4,16,512]{2,1,0:T(8,128)(2,1)S(1)} custom-call(s32[5]{0:T(128)S(1)} %get-tuple-element.17.info_ref, bf16[16,16,512]{2,1,0:T(8,128)(2,1)S(1)} %all-to-all-done.states_ref, f32[16,512]{1,0:T(8,128)} %rates_ref.7), custom_call_target="tpu_custom_call" | custom-call | flops 2097152 | bytes 327680 | tf_op jit(solution)/shard_map/relay/pallas_call | solution.py:287
  41.9 8.5 %all_to_all.19.shares_ref = bf16[4,16,512]{2,1,0:T(8,128)(2,1)S(1)} all-to-all(bf16[4,16,512]{2,1,0:T(8,128)(2,1)S(1)} %relay.1), channel_id=1, replica_groups={{0,128,256,384},{8,136,264,392},{16,144,272,400},{24,152,280,408},{32,1..., dimensions={0} | all-to-all | bytes 131072 | tf_op jit(solution)/shard_map/all_to_all | solution.py:298
  50.3 0.0 all-gather.2.cloned.1.call-done.proj_ref
  50.3 5.5 %hidden.1 = (bf16[256,512]{1,0:T(8,128)(2,1)S(1)}, bf16[256,512]{1,0:T(8,128)(2,1)S(1)}, bf16[1024,4096]{1,0:T(8,128)(2,1)S(1)}) custom-call(s32[5]{0:T(128)S(1)} %get-tuple-element.17.info_ref, bf16[4,16,512]{2,1,0:T(8,128)(2,1)S(1)} %all_to_all.19.shares_ref, f32[16,512]{1,0:T(8,128)} %rates_ref.7, f32[16,512]{1,0:T(8,128)} %residues_ref.3, ...), custom_call_target="tpu_custom_call" | custom-call | flops 12582912 | bytes 2097152 | tf_op jit(solution)/shard_map/hidden/pallas_call | solution.py:300
  55.8 9.5 %collective-permute-start = (bf16[256,512]{1,0:T(8,128)(2,1)S(1)}, bf16[256,512]{1,0:T(8,128)(2,1)S(1)}, u32[]{:S(2)}, u32[]{:S(2)}) collective-permute-start(bf16[256,512]{1,0:T(8,128)(2,1)S(1)} %get-tuple-element.21), channel_id=1, source_target_pairs={{0,1},{1,0},{2,3},{3,2},{4,5},{5,4},{6,7},{7,6},{8,9},{9,8},{10,11... | collective-permute-start | bytes 786440 | tf_op jit(solution)/shard_map/ppermute | solution.py:314
  65.3 1.1 %collective-permute-done.peer_ref = bf16[256,512]{1,0:T(8,128)(2,1)S(1)} collective-permute-done((bf16[256,512]{1,0:T(8,128)(2,1)S(1)}, bf16[256,512]{1,0:T(8,128)(2,1)S(1)}, u32[]{:S(2)}, u32[]{:S(2)}) %collective-permute-start) | collective-permute-done | bytes 262176 | tf_op jit(solution)/shard_map/ppermute | solution.py:314
  66.5 3.8 %project.1 = (bf16[256,4096]{1,0:T(8,128)(2,1)S(1)}, f32[64,4096]{1,0:T(8,128)S(1)}) custom-call(bf16[256,512]{1,0:T(8,128)(2,1)S(1)} %get-tuple-element.20.mine_ref, bf16[256,512]{1,0:T(8,128)(2,1)S(1)} %collective-permute-done.peer_ref, bf16[1024,4096]{1,0:T(8,128)(2,1)S(1)} %get-tuple-element.22.weights_ref), custom_call_target="tpu_custom_call" | custom-call | flops 2147483648 | bytes 8388608 | tf_op jit(solution)/shard_map/project/pallas_call | solution.py:319
  70.3 29.3 %all_to_all.20.pieces_ref = bf16[4,64,4096]{2,1,0:T(8,128)(2,1)S(1)} all-to-all(bf16[4,64,4096]{2,1,0:T(8,128)(2,1)S(1)} %bitcast.2), channel_id=1, replica_groups={{0,2,4,6},{1,3,5,7},{8,10,12,14},{9,11,13,15},{16,18,20,22},{17,19,21,2..., dimensions={0} | all-to-all | bytes 4194304 | tf_op jit(solution)/shard_map/all_to_all | solution.py:333
  99.6 1.2 %total.1 = bf16[64,4096]{1,0:T(8,128)(2,1)} custom-call(bf16[4,64,4096]{2,1,0:T(8,128)(2,1)S(1)} %all_to_all.20.pieces_ref, f32[64,4096]{1,0:T(8,128)S(1)} %get-tuple-element.24.kept_ref), custom_call_target="tpu_custom_call" | custom-call | flops 1048576 | bytes 2097152 | tf_op jit(solution)/shard_map/total/pallas_call | solution.py:336
Async XLA Ops:
  6.5 0.7 copy-start
  6.5 21.0 %copy-start.1 = (f32[512]{0:T(512)S(1)}, f32[512]{0:T(512)}, u32[]{:S(2)}) copy-start(f32[512]{0:T(512)} %param.13) | copy-start | bytes 6148
  6.5 43.8 %all-gather.2.cloned.1.call-start = ((), (), s32[]{:S(2)}) async-start(), calls=%async_computation.3 | async-start | bytes 12582912 | tf_op jit(solution)/shard_map/all_gather | solution.py:242
  11.8 28.9 %all-to-all-start = ((bf16[16,16,512]{2,1,0:T(8,128)(2,1)}), bf16[16,16,512]{2,1,0:T(8,128)(2,1)S(1)}, u32[]{:S(2)}, u32[]{:S(2)}) async-start(bf16[16,16,512]{2,1,0:T(8,128)(2,1)} %get-tuple-element.18), calls=%async_computation | async-start | bytes 524288 | tf_op jit(solution)/shard_map/all_to_all | solution.py:270
  55.8 10.7 %collective-permute-start = (bf16[256,512]{1,0:T(8,128)(2,1)S(1)}, bf16[256,512]{1,0:T(8,128)(2,1)S(1)}, u32[]{:S(2)}, u32[]{:S(2)}) collective-permute-start(bf16[256,512]{1,0:T(8,128)(2,1)S(1)} %get-tuple-element.21), channel_id=1, source_target_pairs={{0,1},{1,0},{2,3},{3,2},{4,5},{5,4},{6,7},{7,6},{8,9},{9,8},{10,11... | collective-permute-start | bytes 786440 | tf_op jit(solution)/shard_map/ppermute | solution.py:314
Sparse Core Ops, SparseCore 0:
  9.4 37.0 all-gather.1

commit v3 on v2

--- a/solution.py
+++ b/solution.py
@@ -31,17 +31,23 @@
     return starts
 
 
-def state_kernel(lengths_ref, gate_ref, signal_ref, rates_ref, feed_ref, enter_ref, send_ref, ends_ref):
+def state_kernel(lengths_ref, gate_ref, signal_ref, rates_ref, feed_ref, enter_ref, send_ref, ends_ref, last_ref):
     length = gate_ref.shape[0]
     modes = rates_ref.shape[0]
     chunk = length // SUB
     begin = lax.axis_index("ctx") * length
     feed_ref[0] = gate_ref[...].astype(F32) * signal_ref[...].astype(F32)
-    chunk_begin = begin + chunk * lax.broadcasted_iota(jnp.int32, (SUB, LANES), 0)
-    last = jnp.full((SUB, LANES), -1, jnp.int32)
-    for start in starts_of(lengths_ref):
-        offset = start - chunk_begin
-        last = jnp.where((offset >= 0) & (offset < chunk), jnp.maximum(last, offset), last)
+
+    @pl.when(pl.program_id(0) == 0)
+    def _():
+        chunk_begin = begin + chunk * lax.broadcasted_iota(jnp.int32, (SUB, LANES), 0)
+        last = jnp.full((SUB, LANES), -1, jnp.int32)
+        for start in starts_of(lengths_ref):
+            offset = start - chunk_begin
+            last = jnp.where((offset >= 0) & (offset < chunk), jnp.maximum(last, offset), last)
+        last_ref[...] = last
+
+    last = last_ref[...]
     whole = (last < 0).astype(F32)
     decay = jnp.exp(-rates_ref[...])
     steps = [jnp.broadcast_to(decay[n : n + 1, :], (SUB, LANES)) for n in range(modes)]
@@ -189,16 +195,7 @@
             copy.wait()
 
 
-def joined(mine, peer, weights_ref, cols):
-    core = lax.axis_index("tp") % CORES
-    depth = mine.shape[1]
-    own = weights_ref[pl.ds(pl.multiple_of(core * depth, depth), depth), cols]
-    far = weights_ref[pl.ds(pl.multiple_of((1 - core) * depth, depth), depth), cols]
-    total = jnp.dot(mine, own, preferred_element_type=F32)
-    return total + jnp.dot(peer, far, preferred_element_type=F32)
-
-
-def project_kernel(mine_ref, peer_ref, weights_ref, out_ref, kept_ref, sums_ref, slots_ref, sems):
+def project_kernel(mine_ref, peer_ref, own_ref, far_ref, out_ref, kept_ref, sums_ref, slots_ref, sems):
     count, _, tile = slots_ref.shape
     keep = kept_ref.shape[0]
     rows = pl.ds(pl.multiple_of(lax.axis_index("tp") // CORES * keep, keep), keep)
@@ -206,7 +203,9 @@
     for j in range(count):
         cols = pl.ds(j * tile, tile)
         sums = sums_ref.at[j % 2]
-        sums[...] = joined(mine_ref[...], peer_ref[...], weights_ref, cols)
+        sums[...] = jnp.dot(mine_ref[...], own_ref[:, cols], preferred_element_type=F32) + jnp.dot(
+            peer_ref[...], far_ref[:, cols], preferred_element_type=F32
+        )
         slots_ref[j] = sums[...].astype(BF16)
         kept_ref[:, cols] = sums[rows, :]
         copies.append(pltpu.make_async_copy(slots_ref.at[j], out_ref.at[:, cols], sems.at[j]))
@@ -238,10 +237,9 @@
     modes = decay_rates.shape[0]
     width = out_proj.shape[1]
     pairs = [(t, t ^ 1) for t in range(lanes)]
-    chip_pairs = [[t, t + 1] for t in range(0, lanes, CORES)]
-    chip_proj = lax.all_gather(out_proj, "tp", axis_index_groups=chip_pairs, tiled=True)
-    gate_out, gate_in, signal, decay_rates, residues, chip_proj = (
-        pltpu.with_memory_space_constraint(v, pltpu.HBM) for v in (gate_out, gate_in, signal, decay_rates, residues, chip_proj)
+    skip_gain = skip_gain.reshape(1, channels)
+    gate_out, gate_in, signal, decay_rates, residues, skip_gain, doc_lengths = (
+        pltpu.with_memory_space_constraint(v, pltpu.HBM) for v in (gate_out, gate_in, signal, decay_rates, residues, skip_gain, doc_lengths)
     )
     tiles = channels // LANES
     columns_y = shards // Z_AXIS
@@ -261,7 +259,7 @@
             jax.ShapeDtypeStruct((tiles, modes * SUB, LANES), F32),
             jax.ShapeDtypeStruct((Z_AXIS, modes, channels), BF16),
         ],
-        scratch_shapes=[pltpu.VMEM((modes * SUB, LANES), F32)],
+        scratch_shapes=[pltpu.VMEM((modes * SUB, LANES), F32), pltpu.VMEM((SUB, LANES), jnp.int32)],
         compiler_params=limit(),
         cost_estimate=cost(4 * length * channels * modes, 3 * length * channels * 4),
     )(doc_lengths, gate_in, signal, decay_rates)
@@ -282,7 +280,11 @@
         scratch_shapes=[pltpu.VMEM((length // SUB, SUB, LANES), F32)],
         compiler_params=limit(),
         cost_estimate=cost(8 * length * channels * modes, 2 * length * channels * 4),
-    )(doc_lengths, feed, enter, decay_rates, residues, skip_gain.reshape(1, channels))
+    )(doc_lengths, feed, enter, decay_rates, residues, skip_gain)
+
+    states, local, out_proj = lax.optimization_barrier((states, local, out_proj))
+    far_proj = lax.ppermute(out_proj, "tp", pairs)
+    out_proj = pltpu.with_memory_space_constraint(out_proj, pltpu.HBM)
 
     shares = pl.pallas_call(
         functools.partial(relay_kernel, length=length),
@@ -305,11 +307,11 @@
                   pl.BlockSpec(memory_space=pl.ANY)],
         out_specs=[columns(half), columns(half), vmem()],
         out_shape=[jax.ShapeDtypeStruct((half, channels), BF16)] * 2
-        + [jax.ShapeDtypeStruct((CORES * channels, width), BF16)],
+        + [jax.ShapeDtypeStruct((channels, width), BF16)],
         scratch_shapes=[pltpu.VMEM((length, LANES), F32), pltpu.SemaphoreType.DMA((4,))],
         compiler_params=limit(),
         cost_estimate=cost(3 * length * channels * modes, 2 * length * channels * 4),
-    )(info, shares, decay_rates, residues, local, gate_out, chip_proj)
+    )(info, shares, decay_rates, residues, local, gate_out, out_proj)
 
     peer = lax.ppermute(other, "tp", pairs)
     chips = lanes // CORES
@@ -319,7 +321,7 @@
     sent, kept = pl.pallas_call(
         project_kernel,
         name="project",
-        in_specs=[vmem(), vmem(), vmem()],
+        in_specs=[vmem()] * 4,
         out_specs=[pl.BlockSpec(memory_space=pl.ANY), vmem()],
         out_shape=[jax.ShapeDtypeStruct((half, width), BF16), jax.ShapeDtypeStruct((keep, width), F32)],
         scratch_shapes=[
@@ -329,7 +331,7 @@
         ],
         compiler_params=limit(16),
         cost_estimate=cost(4 * half * channels * width, 4 * channels * width),
-    )(mine, peer, weights)
+    )(mine, peer, weights, far_proj)
     pieces = lax.all_to_all(sent, "tp", 0, 0, axis_index_groups=chip_groups, tiled=True)
 
     tile = min(2048, width)

time: 108 us -> 94.7 us (0.88)
  between operations: 13.5 us -> 0.06 us
  starting transfers between devices: 25.3 us -> 27.2 us
  Pallas kernels: 23.6 us -> 22.5 us
    ppermute x0 -> x1, starting transfers between devices: none -> 8.08 us  [per_device(): far_proj = lax.ppermute(out_proj, 'tp', pairs)]
    ppermute x1, starting transfers between devices: 9.52 us -> 3.35 us  [per_device(): peer = lax.ppermute(other, 'tp', pairs)]
    pallas_call x1, Pallas kernels: 5.5 us -> 4.31 us  [per_device(): pl.pallas_call(hidden_kernel, name='hidden', grid=(tiles,), in_specs=[sme...]
  transfers between devices with their start and end apart: 3 -> 3, of which waited for: 2 -> 2; matrix products, arithmetic and copies ran while one was open for 0% -> 0% of each run, Pallas kernels for 12% -> 14%
where the time goes in v3:
time: 94.7 us; the launch traced here: 94.2 us
  blocking collectives  37.7 us (40%)
  starting transfers between devices  27.2 us (29%)
  Pallas kernels  22.5 us (24%)
  waiting for transfers between devices  6.76 us (7%)
    all_to_all x1, blocking collectives, per_device(): lax.all_to_all(sent, 'tp', 0, 0, axis_index_groups=chip_groups, tiled=True)  29.3 us
    all_to_all x1, starting transfers between devices, per_device(): lax.all_to_all(send, 'ctx', 0, 0, axis_index_groups=row_groups, tiled=True)  15.7 us
    all_to_all x1, blocking collectives, per_device(): lax.all_to_all(shares, 'ctx', 0, 0, axis_index_groups=column_groups, tile...  8.46 us
    ppermute x1, starting transfers between devices, per_device(): far_proj = lax.ppermute(out_proj, 'tp', pairs)  8.08 us
    pallas_call x1, Pallas kernels, per_device(): pl.pallas_call(local_kernel, name='local', grid=(tiles,), in_specs=[smem(...  7.51 us
    all_to_all x1, waiting for transfers between devices, per_device(): lax.all_to_all(send, 'ctx', 0, 0, axis_index_groups=row_groups, tiled=True)  5.61 us
    pallas_call x1, Pallas kernels, per_device(): pl.pallas_call(state_kernel, name='state', grid=(tiles,), in_specs=[smem(...  4.37 us
    pallas_call x1, Pallas kernels, per_device(): pl.pallas_call(hidden_kernel, name='hidden', grid=(tiles,), in_specs=[sme...  4.31 us
  transfers between devices with their start and end apart: 3, of which 2 were waited for; matrix products, arithmetic and copies ran while one was open for 0% of the time, Pallas kernels for 14%

profile of v3, /device:TPU:1, one launch (start us, length us, event | category | flops | bytes accessed | tf_op | source)
XLA Modules:
  0.0 94.2 jit_solution(5776243322193790897)
XLA Ops:
  0.0 4.4 %state.1 = (f32[4,512,128]{2,1,0:T(8,128)S(1)}, f32[4,128,128]{2,1,0:T(8,128)S(1)}, bf16[16,16,512]{2,1,0:T(8,128)(2,1)}) custom-call(s32[32]{0:T(128)} %lengths_ref.3, bf16[512,512]{1,0:T(8,128)(2,1)} %gate_ref.2, bf16[512,512]{1,0:T(8,128)(2,1)} %signal_ref.1, f32[16,512]{1,0:T(8,128)} %rates_ref.7), custom_call_target="tpu_custom_call" | custom-call | flops 16777216 | bytes 3145728 | tf_op jit(solution)/shard_map/state/pallas_call | solution.py:251
  4.4 15.7 %all-to-all-start = ((bf16[16,16,512]{2,1,0:T(8,128)(2,1)}), bf16[16,16,512]{2,1,0:T(8,128)(2,1)S(1)}, u32[]{:S(2)}, u32[]{:S(2)}) async-start(bf16[16,16,512]{2,1,0:T(8,128)(2,1)} %get-tuple-element.21), calls=%async_computation | async-start | bytes 524288 | tf_op jit(solution)/shard_map/all_to_all | solution.py:268
  20.1 7.5 %local.1 = (f32[4,512,128]{2,1,0:T(8,128)S(1)}, s32[5]{0:T(128)S(1)}) custom-call(s32[32]{0:T(128)} %lengths_ref.3, f32[4,512,128]{2,1,0:T(8,128)S(1)} %get-tuple-element.18.feed_ref, f32[4,128,128]{2,1,0:T(8,128)S(1)} %get-tuple-element.19.enter_ref, f32[16,512]{1,0:T(8,128)} %rates_ref.7, f32[16,512]{1,0:T(8,128)} %residues_ref.3, f32[1,512]{1,0:T(1,128)} %bitcast.3), custom_call_target="tpu_custom_call" | custom-call | flops 33554432 | bytes 2097152 | tf_op jit(solution)/shard_map/local/pallas_call | solution.py:270
  27.6 5.6 %all-to-all-done.states_ref = bf16[16,16,512]{2,1,0:T(8,128)(2,1)S(1)} async-done(((bf16[16,16,512]{2,1,0:T(8,128)(2,1)}), bf16[16,16,512]{2,1,0:T(8,128)(2,1)S(1)}, u32[]{:S(2)}, u32[]{:S(2)}) %all-to-all-start) | async-done | bytes 262176 | tf_op jit(solution)/shard_map/all_to_all | solution.py:268
  33.3 8.1 %collective-permute-start.1 = (bf16[512,4096]{1,0:T(8,128)(2,1)}, bf16[512,4096]{1,0:T(8,128)(2,1)S(1)}, u32[]{:S(2)}, u32[]{:S(2)}) collective-permute-start(bf16[512,4096]{1,0:T(8,128)(2,1)} %proj_ref), channel_id=1, source_target_pairs={{0,1},{1,0},{2,3},{3,2},{4,5},{5,4},{6,7},{7,6},{8,9},{9,8},{10,11... | collective-permute-start | bytes 12582920 | tf_op jit(solution)/shard_map/ppermute | solution.py:286
  41.3 1.2 %relay.1 = bf16[4,16,512]{2,1,0:T(8,128)(2,1)S(1)} custom-call(s32[5]{0:T(128)S(1)} %get-tuple-element.20.info_ref, bf16[16,16,512]{2,1,0:T(8,128)(2,1)S(1)} %all-to-all-done.states_ref, f32[16,512]{1,0:T(8,128)} %rates_ref.7), custom_call_target="tpu_custom_call" | custom-call | flops 2097152 | bytes 327680 | tf_op jit(solution)/shard_map/relay/pallas_call | solution.py:289
  42.6 8.5 %all_to_all.19.shares_ref = bf16[4,16,512]{2,1,0:T(8,128)(2,1)S(1)} all-to-all(bf16[4,16,512]{2,1,0:T(8,128)(2,1)S(1)} %relay.1), channel_id=1, replica_groups={{0,128,256,384},{8,136,264,392},{16,144,272,400},{24,152,280,408},{32,1..., dimensions={0} | all-to-all | bytes 131072 | tf_op jit(solution)/shard_map/all_to_all | solution.py:300
  51.0 4.3 %hidden.1 = (bf16[256,512]{1,0:T(8,128)(2,1)S(1)}, bf16[256,512]{1,0:T(8,128)(2,1)S(1)}, bf16[512,4096]{1,0:T(8,128)(2,1)S(1)}) custom-call(s32[5]{0:T(128)S(1)} %get-tuple-element.20.info_ref, bf16[4,16,512]{2,1,0:T(8,128)(2,1)S(1)} %all_to_all.19.shares_ref, f32[16,512]{1,0:T(8,128)} %rates_ref.7, f32[16,512]{1,0:T(8,128)} %residues_ref.3, ...), custom_call_target="tpu_custom_call" | custom-call | flops 12582912 | bytes 2097152 | tf_op jit(solution)/shard_map/hidden/pallas_call | solution.py:302
  55.3 3.4 %collective-permute-start = (bf16[256,512]{1,0:T(8,128)(2,1)S(1)}, bf16[256,512]{1,0:T(8,128)(2,1)S(1)}, u32[]{:S(2)}, u32[]{:S(2)}) collective-permute-start(bf16[256,512]{1,0:T(8,128)(2,1)S(1)} %get-tuple-element.27), channel_id=1, source_target_pairs={{0,1},{1,0},{2,3},{3,2},{4,5},{5,4},{6,7},{7,6},{8,9},{9,8},{10,11... | collective-permute-start | bytes 786440 | tf_op jit(solution)/shard_map/ppermute | solution.py:316
  58.7 1.1 %collective-permute-done.peer_ref = bf16[256,512]{1,0:T(8,128)(2,1)S(1)} collective-permute-done((bf16[256,512]{1,0:T(8,128)(2,1)S(1)}, bf16[256,512]{1,0:T(8,128)(2,1)S(1)}, u32[]{:S(2)}, u32[]{:S(2)}) %collective-permute-start) | collective-permute-done | bytes 262176 | tf_op jit(solution)/shard_map/ppermute | solution.py:316
  59.8 0.0 collective-permute-done.1.far_ref
  59.8 3.9 %project.1 = (bf16[256,4096]{1,0:T(8,128)(2,1)S(1)}, f32[64,4096]{1,0:T(8,128)S(1)}) custom-call(bf16[256,512]{1,0:T(8,128)(2,1)S(1)} %get-tuple-element.26.mine_ref, bf16[256,512]{1,0:T(8,128)(2,1)S(1)} %collective-permute-done.peer_ref, bf16[512,4096]{1,0:T(8,128)(2,1)S(1)} %get-tuple-element.28.own_ref, bf16[512,4096]{1,0:T(8,128)(2,1)S(1)} %collective-permute-done.1.far_ref), custom_call_target="tpu_custom_call" | custom-call | flops 2147483648 | bytes 8388608 | tf_op jit(solution)/shard_map/project/pallas_call | solution.py:321
  63.7 29.3 %all_to_all.20.pieces_ref = bf16[4,64,4096]{2,1,0:T(8,128)(2,1)S(1)} all-to-all(bf16[4,64,4096]{2,1,0:T(8,128)(2,1)S(1)} %bitcast.2), channel_id=1, replica_groups={{0,2,4,6},{1,3,5,7},{8,10,12,14},{9,11,13,15},{16,18,20,22},{17,19,21,2..., dimensions={0} | all-to-all | bytes 4194304 | tf_op jit(solution)/shard_map/all_to_all | solution.py:335
  93.0 1.2 %total.1 = bf16[64,4096]{1,0:T(8,128)(2,1)} custom-call(bf16[4,64,4096]{2,1,0:T(8,128)(2,1)S(1)} %all_to_all.20.pieces_ref, f32[64,4096]{1,0:T(8,128)S(1)} %get-tuple-element.30.kept_ref), custom_call_target="tpu_custom_call" | custom-call | flops 1048576 | bytes 2097152 | tf_op jit(solution)/shard_map/total/pallas_call | solution.py:338
Async XLA Ops:
  4.4 28.9 %all-to-all-start = ((bf16[16,16,512]{2,1,0:T(8,128)(2,1)}), bf16[16,16,512]{2,1,0:T(8,128)(2,1)S(1)}, u32[]{:S(2)}, u32[]{:S(2)}) async-start(bf16[16,16,512]{2,1,0:T(8,128)(2,1)} %get-tuple-element.21), calls=%async_computation | async-start | bytes 524288 | tf_op jit(solution)/shard_map/all_to_all | solution.py:268
  33.3 26.6 %collective-permute-start.1 = (bf16[512,4096]{1,0:T(8,128)(2,1)}, bf16[512,4096]{1,0:T(8,128)(2,1)S(1)}, u32[]{:S(2)}, u32[]{:S(2)}) collective-permute-start(bf16[512,4096]{1,0:T(8,128)(2,1)} %proj_ref), channel_id=1, source_target_pairs={{0,1},{1,0},{2,3},{3,2},{4,5},{5,4},{6,7},{7,6},{8,9},{9,8},{10,11... | collective-permute-start | bytes 12582920 | tf_op jit(solution)/shard_map/ppermute | solution.py:286
  55.3 4.5 %collective-permute-start = (bf16[256,512]{1,0:T(8,128)(2,1)S(1)}, bf16[256,512]{1,0:T(8,128)(2,1)S(1)}, u32[]{:S(2)}, u32[]{:S(2)}) collective-permute-start(bf16[256,512]{1,0:T(8,128)(2,1)S(1)} %get-tuple-element.27), channel_id=1, source_target_pairs={{0,1},{1,0},{2,3},{3,2},{4,5},{5,4},{6,7},{7,6},{8,9},{9,8},{10,11... | collective-permute-start | bytes 786440 | tf_op jit(solution)/shard_map/ppermute | solution.py:316

commit v4 on v3

--- a/solution.py
+++ b/solution.py
@@ -31,48 +31,65 @@
     return starts
 
 
-def state_kernel(lengths_ref, gate_ref, signal_ref, rates_ref, feed_ref, enter_ref, send_ref, ends_ref, last_ref):
-    length = gate_ref.shape[0]
+def state_kernel(
+    lengths_ref, gate_hbm, signal_hbm, rates_hbm, feed_ref, enter_ref, send_out,
+    gate_ref, signal_ref, rates_ref, send_ref, ends_ref, in_sems, rates_sem, out_sem,
+):
+    tiles, length, _ = feed_ref.shape
     modes = rates_ref.shape[0]
     chunk = length // SUB
     begin = lax.axis_index("ctx") * length
-    feed_ref[0] = gate_ref[...].astype(F32) * signal_ref[...].astype(F32)
-
-    @pl.when(pl.program_id(0) == 0)
-    def _():
-        chunk_begin = begin + chunk * lax.broadcasted_iota(jnp.int32, (SUB, LANES), 0)
-        last = jnp.full((SUB, LANES), -1, jnp.int32)
-        for start in starts_of(lengths_ref):
-            offset = start - chunk_begin
-            last = jnp.where((offset >= 0) & (offset < chunk), jnp.maximum(last, offset), last)
-        last_ref[...] = last
-
-    last = last_ref[...]
+    rates_copy = pltpu.make_async_copy(rates_hbm, rates_ref, rates_sem)
+    copies = []
+    for g in range(tiles):
+        cols = pl.ds(g * LANES, LANES)
+        copies.append(pltpu.make_async_copy(gate_hbm.at[:, cols], gate_ref.at[g], in_sems.at[0, g]))
+        copies.append(pltpu.make_async_copy(signal_hbm.at[:, cols], signal_ref.at[g], in_sems.at[1, g]))
+    copies[0].start()
+    copies[1].start()
+    rates_copy.start()
+    for copy in copies[2:]:
+        copy.start()
+    chunk_begin = begin + chunk * lax.broadcasted_iota(jnp.int32, (SUB, LANES), 0)
+    last = jnp.full((SUB, LANES), -1, jnp.int32)
+    for start in starts_of(lengths_ref):
+        offset = start - chunk_begin
+        last = jnp.where((offset >= 0) & (offset < chunk), jnp.maximum(last, offset), last)
     whole = (last < 0).astype(F32)
-    decay = jnp.exp(-rates_ref[...])
-    steps = [jnp.broadcast_to(decay[n : n + 1, :], (SUB, LANES)) for n in range(modes)]
-
-    def advance(i, states):
-        row = feed_ref[0, pl.ds(i, SUB, stride=chunk), :]
-        row = jnp.where(last <= i, row, 0.0)
-        return tuple(s * a + row for s, a in zip(states, steps))
-
-    zero = jnp.zeros((SUB, LANES), F32)
-    states = lax.fori_loop(0, chunk, advance, (zero,) * modes, unroll=4)
-    for n in range(modes):
-        ends_ref[SUB * n : SUB * n + SUB, :] = states[n]
-    chunk_decay = jnp.exp(-float(chunk) * rates_ref[...])
-    carry = jnp.zeros((modes, LANES), F32)
-    for s in range(SUB):
-        enter_ref[0, pl.ds(s, modes, stride=SUB), :] = carry
-        passed = jnp.broadcast_to(whole[s : s + 1, :], (modes, LANES))
-        carry = carry * chunk_decay * passed + ends_ref[pl.ds(s, modes, stride=SUB), :]
-    rounded = carry.astype(BF16)
-    for r in range(send_ref.shape[0]):
-        send_ref[r] = rounded
-
-
-def local_kernel(lengths_ref, feed_ref, enter_ref, rates_ref, residues_ref, skip_ref, out_ref, info_ref, mark_ref):
+    rates_copy.wait()
+    for g in range(tiles):
+        copies[2 * g].wait()
+        copies[2 * g + 1].wait()
+        rates = rates_ref[:, g * LANES : g * LANES + LANES]
+        decay = jnp.exp(-rates)
+        steps = [jnp.broadcast_to(decay[n : n + 1, :], (SUB, LANES)) for n in range(modes)]
+        feed_ref[g] = gate_ref[g].astype(F32) * signal_ref[g].astype(F32)
+
+        def advance(i, states, g=g, steps=steps):
+            row = feed_ref[g, pl.ds(i, SUB, stride=chunk), :]
+            row = jnp.where(last <= i, row, 0.0)
+            return tuple(s * a + row for s, a in zip(states, steps))
+
+        zero = jnp.zeros((SUB, LANES), F32)
+        states = lax.fori_loop(0, chunk, advance, (zero,) * modes, unroll=8)
+        for n in range(modes):
+            ends_ref[g, SUB * n : SUB * n + SUB, :] = states[n]
+    for g in range(tiles):
+        chunk_decay = jnp.exp(-float(chunk) * rates_ref[:, g * LANES : g * LANES + LANES])
+        carry = jnp.zeros((modes, LANES), F32)
+        for s in range(SUB):
+            enter_ref[g, pl.ds(s, modes, stride=SUB), :] = carry
+            passed = jnp.broadcast_to(whole[s : s + 1, :], (modes, LANES))
+            carry = carry * chunk_decay * passed + ends_ref[g, pl.ds(s, modes, stride=SUB), :]
+        rounded = carry.astype(BF16)
+        for r in range(send_ref.shape[0]):
+            send_ref[r, :, g * LANES : g * LANES + LANES] = rounded
+    out = pltpu.make_async_copy(send_ref, send_out, out_sem)
+    out.start()
+    out.wait()
+
+
+def local_kernel(lengths_ref, feed_ref, enter_ref, rates_ref, residues_ref, skip_ref, out_ref, info_ref, decay_ref, entry_ref, mark_ref):
     length = feed_ref.shape[1]
     modes = rates_ref.shape[0]
     chunk = length // SUB
@@ -106,6 +123,12 @@
     decay = jnp.exp(-rates_ref[...])
     steps = [jnp.broadcast_to(decay[n : n + 1, :], (SUB, LANES)) for n in range(modes)]
     skip = jnp.broadcast_to(skip_ref[...], (SUB, LANES))
+    decay_ref[...] = decay
+    ages = (chunk * lax.broadcasted_iota(jnp.int32, (SUB, LANES), 0)).astype(F32)
+    for n in range(modes):
+        rate = jnp.broadcast_to(rates_ref[n : n + 1, :], (SUB, LANES))
+        weight = jnp.broadcast_to(residues_ref[n : n + 1, :], (SUB, LANES))
+        entry_ref[0, SUB * n : SUB * n + SUB, :] = jnp.exp(-ages * rate) * weight
 
     def advance(i, states):
         fed = feed_ref[0, pl.ds(i, SUB, stride=chunk), :]
@@ -141,58 +164,56 @@
 
 
 def hidden_kernel(
-    info_ref, shares_ref, rates_ref, residues_ref, local_ref, gate_ref, proj_ref,
-    mine_ref, other_ref, weights_ref, prior_ref, sems,
+    info_ref, shares_ref, decay_ref, entry_ref, local_ref, gate_hbm, proj_hbm,
+    mine_ref, other_ref, weights_ref, gate_ref, prior_ref, carry_ref, gate_sems, sems,
 ):
-    length = gate_ref.shape[0]
+    tiles, length, _ = local_ref.shape
+    modes = decay_ref.shape[0]
+    chunk = length // SUB
+    copies = []
+    for g in range(tiles):
+        cols = pl.ds(g * LANES, LANES)
+        copies.append(pltpu.make_async_copy(gate_hbm.at[:, cols], gate_ref.at[g], gate_sems.at[g]))
     count = sems.shape[0]
-    depth = proj_ref.shape[0] // count
-    copies = [
-        pltpu.make_async_copy(proj_ref.at[pl.ds(i * depth, depth)], weights_ref.at[pl.ds(i * depth, depth)], sems.at[i])
+    depth = proj_hbm.shape[0] // count
+    moves = [
+        pltpu.make_async_copy(proj_hbm.at[pl.ds(i * depth, depth)], weights_ref.at[pl.ds(i * depth, depth)], sems.at[i])
         for i in range(count)
     ]
-
-    @pl.when(pl.program_id(0) == 0)
-    def _():
-        for copy in copies:
-            copy.start()
-
-    modes = rates_ref.shape[0]
-    chunk = length // SUB
+    for copy in copies + moves:
+        copy.start()
     carried = shares_ref[0].astype(F32)
     for g in range(1, shares_ref.shape[0]):
         carried = carried + shares_ref[g].astype(F32)
-    carried = carried * residues_ref[...]
-    decay = jnp.exp(-rates_ref[...])
+    carry_ref[...] = carried
     chunk_begin = chunk * lax.broadcasted_iota(jnp.int32, (SUB, LANES), 0)
     ahead = info_ref[0] - chunk_begin
-    ages = chunk_begin.astype(F32)
-    steps = [jnp.broadcast_to(decay[n : n + 1, :], (SUB, LANES)) for n in range(modes)]
-
-    def advance(i, states):
-        new = tuple(s * a for s, a in zip(states, steps))
-        sums = list(new)
-        while len(sums) > 1:
-            sums = [sums[k] + sums[k + 1] for k in range(0, len(sums), 2)]
-        prior_ref[pl.ds(i, SUB, stride=chunk), :] = jnp.where(ahead > i, sums[0], 0.0)
-        return new
-
-    init = []
-    for n in range(modes):
-        rate = jnp.broadcast_to(rates_ref[n : n + 1, :], (SUB, LANES))
-        init.append(jnp.exp(-ages * rate) * jnp.broadcast_to(carried[n : n + 1, :], (SUB, LANES)))
-    lax.fori_loop(0, chunk, advance, tuple(init), unroll=4)
     core = lax.axis_index("tp") % CORES
-    for x in range(SUB // CORES):
-        for side, ref in ((core, mine_ref), (1 - core, other_ref)):
-            rows = pl.ds(pl.multiple_of((x * CORES + side) * chunk, chunk), chunk)
-            mixed = local_ref[0, rows, :] + prior_ref[rows, :]
-            ref[x * chunk : (x + 1) * chunk, :] = (gate_ref[rows, :].astype(F32) * mixed).astype(BF16)
-
-    @pl.when(pl.program_id(0) == pl.num_programs(0) - 1)
-    def _():
-        for copy in copies:
-            copy.wait()
+    for g in range(tiles):
+        part = slice(g * LANES, g * LANES + LANES)
+        steps = [jnp.broadcast_to(decay_ref[n : n + 1, part], (SUB, LANES)) for n in range(modes)]
+        init = [
+            entry_ref[g, SUB * n : SUB * n + SUB, :] * jnp.broadcast_to(carry_ref[n : n + 1, part], (SUB, LANES))
+            for n in range(modes)
+        ]
+
+        def advance(i, states, g=g, steps=steps):
+            new = tuple(s * a for s, a in zip(states, steps))
+            sums = list(new)
+            while len(sums) > 1:
+                sums = [sums[k] + sums[k + 1] for k in range(0, len(sums), 2)]
+            prior_ref[g, pl.ds(i, SUB, stride=chunk), :] = jnp.where(ahead > i, sums[0], 0.0)
+            return new
+
+        lax.fori_loop(0, chunk, advance, tuple(init), unroll=8)
+        copies[g].wait()
+        for x in range(SUB // CORES):
+            for side, ref in ((core, mine_ref), (1 - core, other_ref)):
+                rows = pl.ds(pl.multiple_of((x * CORES + side) * chunk, chunk), chunk)
+                mixed = local_ref[g, rows, :] + prior_ref[g, rows, :]
+                ref[x * chunk : (x + 1) * chunk, part] = (gate_ref[g, rows, :].astype(F32) * mixed).astype(BF16)
+    for move in moves:
+        move.wait()
 
 
 def project_kernel(mine_ref, peer_ref, own_ref, far_ref, out_ref, kept_ref, sums_ref, slots_ref, sems):
@@ -246,20 +267,28 @@
     half = length // CORES
     columns = lambda rows: pl.BlockSpec((rows, LANES), lambda g: (0, g))
     stack = lambda rows: pl.BlockSpec((1, rows, LANES), lambda g: (g, 0, 0))
-    pages = lambda count: pl.BlockSpec((count, modes, LANES), lambda g: (0, 0, g))
-
+
+    anywhere = pl.BlockSpec(memory_space=pl.ANY)
     feed, enter, send = pl.pallas_call(
         state_kernel,
         name="state",
-        grid=(tiles,),
-        in_specs=[smem(), columns(length), columns(length), columns(modes)],
-        out_specs=[stack(length), stack(modes * SUB), pages(Z_AXIS)],
+        in_specs=[smem(), anywhere, anywhere, anywhere],
+        out_specs=[vmem(), vmem(), anywhere],
         out_shape=[
             jax.ShapeDtypeStruct((tiles, length, LANES), F32),
             jax.ShapeDtypeStruct((tiles, modes * SUB, LANES), F32),
             jax.ShapeDtypeStruct((Z_AXIS, modes, channels), BF16),
         ],
-        scratch_shapes=[pltpu.VMEM((modes * SUB, LANES), F32), pltpu.VMEM((SUB, LANES), jnp.int32)],
+        scratch_shapes=[
+            pltpu.VMEM((tiles, length, LANES), BF16),
+            pltpu.VMEM((tiles, length, LANES), BF16),
+            pltpu.VMEM((modes, channels), F32),
+            pltpu.VMEM((Z_AXIS, modes, channels), BF16),
+            pltpu.VMEM((tiles, modes * SUB, LANES), F32),
+            pltpu.SemaphoreType.DMA((2, tiles)),
+            pltpu.SemaphoreType.DMA,
+            pltpu.SemaphoreType.DMA,
+        ],
         compiler_params=limit(),
         cost_estimate=cost(4 * length * channels * modes, 3 * length * channels * 4),
     )(doc_lengths, gate_in, signal, decay_rates)
@@ -267,15 +296,17 @@
     row_groups = [[y * Z_AXIS + z for z in range(Z_AXIS)] for y in range(columns_y)]
     states = lax.all_to_all(send, "ctx", 0, 0, axis_index_groups=row_groups, tiled=True)
 
-    local, info = pl.pallas_call(
+    local, info, decay, entry = pl.pallas_call(
         local_kernel,
         name="local",
         grid=(tiles,),
         in_specs=[smem(), stack(length), stack(modes * SUB), columns(modes), columns(modes), columns(1)],
-        out_specs=[stack(length), smem()],
+        out_specs=[stack(length), smem(), columns(modes), stack(modes * SUB)],
         out_shape=[
             jax.ShapeDtypeStruct((tiles, length, LANES), F32),
             jax.ShapeDtypeStruct((1 + columns_y,), jnp.int32),
+            jax.ShapeDtypeStruct((modes, channels), F32),
+            jax.ShapeDtypeStruct((tiles, modes * SUB, LANES), F32),
         ],
         scratch_shapes=[pltpu.VMEM((length // SUB, SUB, LANES), F32)],
         compiler_params=limit(),
@@ -302,16 +333,20 @@
     mine, other, weights = pl.pallas_call(
         hidden_kernel,
         name="hidden",
-        grid=(tiles,),
-        in_specs=[smem(), pages(columns_y), columns(modes), columns(modes), stack(length), columns(length),
-                  pl.BlockSpec(memory_space=pl.ANY)],
-        out_specs=[columns(half), columns(half), vmem()],
+        in_specs=[smem(), vmem(), vmem(), vmem(), vmem(), anywhere, anywhere],
+        out_specs=[vmem()] * 3,
         out_shape=[jax.ShapeDtypeStruct((half, channels), BF16)] * 2
         + [jax.ShapeDtypeStruct((channels, width), BF16)],
-        scratch_shapes=[pltpu.VMEM((length, LANES), F32), pltpu.SemaphoreType.DMA((4,))],
+        scratch_shapes=[
+            pltpu.VMEM((tiles, length, LANES), BF16),
+            pltpu.VMEM((tiles, length, LANES), F32),
+            pltpu.VMEM((modes, channels), F32),
+            pltpu.SemaphoreType.DMA((tiles,)),
+            pltpu.SemaphoreType.DMA((4,)),
+        ],
         compiler_params=limit(),
         cost_estimate=cost(3 * length * channels * modes, 2 * length * channels * 4),
-    )(info, shares, decay_rates, residues, local, gate_out, out_proj)
+    )(info, shares, decay, entry, local, gate_out, out_proj)
 
     peer = lax.ppermute(other, "tp", pairs)
     chips = lanes // CORES

time: 94.7 us -> 93.4 us (0.986)
  Pallas kernels: 22.5 us -> 21.3 us
    pallas_call x2, Pallas kernels: 8.68 us -> 7.52 us  [the longest x1 4.52 us: per_device(): pl.pallas_call(state_kernel, name='state', in_specs=[smem(), anywhere, an...]
  transfers between devices with their start and end apart: 3 -> 3, of which waited for: 2 -> 2; matrix products, arithmetic and copies ran while one was open for 0% -> 0% of each run, Pallas kernels for 14% -> 13%
where the time goes in v4:
time: 93.4 us; the launch traced here: 93 us
  blocking collectives  37.7 us (40%)
  starting transfers between devices  27.2 us (29%)
  Pallas kernels  21.3 us (23%)
  waiting for transfers between devices  6.69 us (7%)
    all_to_all x1, blocking collectives, per_device(): lax.all_to_all(sent, 'tp', 0, 0, axis_index_groups=chip_groups, tiled=True)  29.3 us
    all_to_all x1, starting transfers between devices, per_device(): lax.all_to_all(send, 'ctx', 0, 0, axis_index_groups=row_groups, tiled=True)  15.8 us
    all_to_all x1, blocking collectives, per_device(): lax.all_to_all(shares, 'ctx', 0, 0, axis_index_groups=column_groups, tile...  8.46 us
    ppermute x1, starting transfers between devices, per_device(): far_proj = lax.ppermute(out_proj, 'tp', pairs)  8.08 us
    pallas_call x1, Pallas kernels, per_device(): pl.pallas_call(local_kernel, name='local', grid=(tiles,), in_specs=[smem(...  7.58 us
    all_to_all x1, waiting for transfers between devices, per_device(): lax.all_to_all(send, 'ctx', 0, 0, axis_index_groups=row_groups, tiled=True)  5.54 us
    pallas_call x1, Pallas kernels, per_device(): pl.pallas_call(state_kernel, name='state', in_specs=[smem(), anywhere, an...  4.52 us
    pallas_call x1, Pallas kernels, per_device(): pl.pallas_call(project_kernel, name='project', in_specs=[vmem()] * 4, out...  3.82 us
  transfers between devices with their start and end apart: 3, of which 2 were waited for; matrix products, arithmetic and copies ran while one was open for 0% of the time, Pallas kernels for 13%

profile of v4, /device:TPU:1, one launch (start us, length us, event | category | flops | bytes accessed | tf_op | source)
XLA Modules:
  0.0 93.0 jit_solution(17867605627958161428)
XLA Ops:
  0.0 4.5 %state.1 = (f32[4,512,128]{2,1,0:T(8,128)S(1)}, f32[4,128,128]{2,1,0:T(8,128)S(1)}, bf16[16,16,512]{2,1,0:T(8,128)(2,1)}) custom-call(s32[32]{0:T(128)} %lengths_ref.3, bf16[512,512]{1,0:T(8,128)(2,1)} %gate_hbm.2, bf16[512,512]{1,0:T(8,128)(2,1)} %signal_hbm.1, f32[16,512]{1,0:T(8,128)} %rates_ref.3), custom_call_target="tpu_custom_call" | custom-call | flops 16777216 | bytes 3145728 | tf_op jit(solution)/shard_map/state/pallas_call | solution.py:272
  4.5 15.8 %all-to-all-start = ((bf16[16,16,512]{2,1,0:T(8,128)(2,1)}), bf16[16,16,512]{2,1,0:T(8,128)(2,1)S(1)}, u32[]{:S(2)}, u32[]{:S(2)}) async-start(bf16[16,16,512]{2,1,0:T(8,128)(2,1)} %get-tuple-element.23), calls=%async_computation | async-start | bytes 524288 | tf_op jit(solution)/shard_map/all_to_all | solution.py:297
  20.3 7.6 %local.1 = (f32[4,512,128]{2,1,0:T(8,128)S(1)}, s32[5]{0:T(128)S(1)}, f32[16,512]{1,0:T(8,128)S(1)}, f32[4,128,128]{2,1,0:T(8,128)S(1)}) custom-call(s32[32]{0:T(128)} %lengths_ref.3, f32[4,512,128]{2,1,0:T(8,128)S(1)} %get-tuple-element.20.feed_ref, f32[4,128,128]{2,1,0:T(8,128)S(1)} %get-tuple-element.21.enter_ref, f32[16,512]{1,0:T(8,128)} %rates_ref.3, ...), custom_call_target="tpu_custom_call" | custom-call | flops 33554432 | bytes 2097152 | tf_op jit(solution)/shard_map/local/pallas_call | solution.py:299
  27.9 5.5 %all-to-all-done.states_ref = bf16[16,16,512]{2,1,0:T(8,128)(2,1)S(1)} async-done(((bf16[16,16,512]{2,1,0:T(8,128)(2,1)}), bf16[16,16,512]{2,1,0:T(8,128)(2,1)S(1)}, u32[]{:S(2)}, u32[]{:S(2)}) %all-to-all-start) | async-done | bytes 262176 | tf_op jit(solution)/shard_map/all_to_all | solution.py:297
  33.4 8.1 %collective-permute-start.1 = (bf16[512,4096]{1,0:T(8,128)(2,1)}, bf16[512,4096]{1,0:T(8,128)(2,1)S(1)}, u32[]{:S(2)}, u32[]{:S(2)}) collective-permute-start(bf16[512,4096]{1,0:T(8,128)(2,1)} %proj_hbm), channel_id=1, source_target_pairs={{0,1},{1,0},{2,3},{3,2},{4,5},{5,4},{6,7},{7,6},{8,9},{9,8},{10,11... | collective-permute-start | bytes 12582920 | tf_op jit(solution)/shard_map/ppermute | solution.py:317
  41.5 1.2 %relay.1 = bf16[4,16,512]{2,1,0:T(8,128)(2,1)S(1)} custom-call(s32[5]{0:T(128)S(1)} %get-tuple-element.22.info_ref, bf16[16,16,512]{2,1,0:T(8,128)(2,1)S(1)} %all-to-all-done.states_ref, f32[16,512]{1,0:T(8,128)} %rates_ref.3), custom_call_target="tpu_custom_call" | custom-call | flops 2097152 | bytes 327680 | tf_op jit(solution)/shard_map/relay/pallas_call | solution.py:320
  42.7 8.5 %all_to_all.19.shares_ref = bf16[4,16,512]{2,1,0:T(8,128)(2,1)S(1)} all-to-all(bf16[4,16,512]{2,1,0:T(8,128)(2,1)S(1)} %relay.1), channel_id=1, replica_groups={{0,128,256,384},{8,136,264,392},{16,144,272,400},{24,152,280,408},{32,1..., dimensions={0} | all-to-all | bytes 131072 | tf_op jit(solution)/shard_map/all_to_all | solution.py:331
  51.2 3.0 %hidden.1 = (bf16[256,512]{1,0:T(8,128)(2,1)S(1)}, bf16[256,512]{1,0:T(8,128)(2,1)S(1)}, bf16[512,4096]{1,0:T(8,128)(2,1)S(1)}) custom-call(s32[5]{0:T(128)S(1)} %get-tuple-element.22.info_ref, bf16[4,16,512]{2,1,0:T(8,128)(2,1)S(1)} %all_to_all.19.shares_ref, f32[16,512]{1,0:T(8,128)S(1)} %get-tuple-element.26.decay_ref, ...), custom_call_target="tpu_custom_call" | custom-call | flops 12582912 | bytes 2097152 | tf_op jit(solution)/shard_map/hidden/pallas_call | solution.py:333
  54.2 3.4 %collective-permute-start = (bf16[256,512]{1,0:T(8,128)(2,1)S(1)}, bf16[256,512]{1,0:T(8,128)(2,1)S(1)}, u32[]{:S(2)}, u32[]{:S(2)}) collective-permute-start(bf16[256,512]{1,0:T(8,128)(2,1)S(1)} %get-tuple-element.31), channel_id=1, source_target_pairs={{0,1},{1,0},{2,3},{3,2},{4,5},{5,4},{6,7},{7,6},{8,9},{9,8},{10,11... | collective-permute-start | bytes 786440 | tf_op jit(solution)/shard_map/ppermute | solution.py:351
  57.5 1.1 %collective-permute-done.peer_ref = bf16[256,512]{1,0:T(8,128)(2,1)S(1)} collective-permute-done((bf16[256,512]{1,0:T(8,128)(2,1)S(1)}, bf16[256,512]{1,0:T(8,128)(2,1)S(1)}, u32[]{:S(2)}, u32[]{:S(2)}) %collective-permute-start) | collective-permute-done | bytes 262176 | tf_op jit(solution)/shard_map/ppermute | solution.py:351
  58.7 0.0 collective-permute-done.1.far_ref
  58.7 3.8 %project.1 = (bf16[256,4096]{1,0:T(8,128)(2,1)S(1)}, f32[64,4096]{1,0:T(8,128)S(1)}) custom-call(bf16[256,512]{1,0:T(8,128)(2,1)S(1)} %get-tuple-element.30.mine_ref, bf16[256,512]{1,0:T(8,128)(2,1)S(1)} %collective-permute-done.peer_ref, bf16[512,4096]{1,0:T(8,128)(2,1)S(1)} %get-tuple-element.32.own_ref, bf16[512,4096]{1,0:T(8,128)(2,1)S(1)} %collective-permute-done.1.far_ref), custom_call_target="tpu_custom_call" | custom-call | flops 2147483648 | bytes 8388608 | tf_op jit(solution)/shard_map/project/pallas_call | solution.py:356
  62.5 29.3 %all_to_all.20.pieces_ref = bf16[4,64,4096]{2,1,0:T(8,128)(2,1)S(1)} all-to-all(bf16[4,64,4096]{2,1,0:T(8,128)(2,1)S(1)} %bitcast.2), channel_id=1, replica_groups={{0,2,4,6},{1,3,5,7},{8,10,12,14},{9,11,13,15},{16,18,20,22},{17,19,21,2..., dimensions={0} | all-to-all | bytes 4194304 | tf_op jit(solution)/shard_map/all_to_all | solution.py:370
  91.8 1.2 %total.1 = bf16[64,4096]{1,0:T(8,128)(2,1)} custom-call(bf16[4,64,4096]{2,1,0:T(8,128)(2,1)S(1)} %all_to_all.20.pieces_ref, f32[64,4096]{1,0:T(8,128)S(1)} %get-tuple-element.34.kept_ref), custom_call_target="tpu_custom_call" | custom-call | flops 1048576 | bytes 2097152 | tf_op jit(solution)/shard_map/total/pallas_call | solution.py:373
Async XLA Ops:
  4.5 28.9 %all-to-all-start = ((bf16[16,16,512]{2,1,0:T(8,128)(2,1)}), bf16[16,16,512]{2,1,0:T(8,128)(2,1)S(1)}, u32[]{:S(2)}, u32[]{:S(2)}) async-start(bf16[16,16,512]{2,1,0:T(8,128)(2,1)} %get-tuple-element.23), calls=%async_computation | async-start | bytes 524288 | tf_op jit(solution)/shard_map/all_to_all | solution.py:297
  33.4 25.3 %collective-permute-start.1 = (bf16[512,4096]{1,0:T(8,128)(2,1)}, bf16[512,4096]{1,0:T(8,128)(2,1)S(1)}, u32[]{:S(2)}, u32[]{:S(2)}) collective-permute-start(bf16[512,4096]{1,0:T(8,128)(2,1)} %proj_hbm), channel_id=1, source_target_pairs={{0,1},{1,0},{2,3},{3,2},{4,5},{5,4},{6,7},{7,6},{8,9},{9,8},{10,11... | collective-permute-start | bytes 12582920 | tf_op jit(solution)/shard_map/ppermute | solution.py:317
  54.2 4.5 %collective-permute-start = (bf16[256,512]{1,0:T(8,128)(2,1)S(1)}, bf16[256,512]{1,0:T(8,128)(2,1)S(1)}, u32[]{:S(2)}, u32[]{:S(2)}) collective-permute-start(bf16[256,512]{1,0:T(8,128)(2,1)S(1)} %get-tuple-element.31), channel_id=1, source_target_pairs={{0,1},{1,0},{2,3},{3,2},{4,5},{5,4},{6,7},{7,6},{8,9},{9,8},{10,11... | collective-permute-start | bytes 786440 | tf_op jit(solution)/shard_map/ppermute | solution.py:351

commit v5 on v4

--- a/solution.py
+++ b/solution.py
@@ -216,32 +216,26 @@
         move.wait()
 
 
-def project_kernel(mine_ref, peer_ref, own_ref, far_ref, out_ref, kept_ref, sums_ref, slots_ref, sems):
+def project_kernel(mine_ref, peer_ref, own_ref, far_ref, out_ref, slots_ref, sems):
     count, _, tile = slots_ref.shape
-    keep = kept_ref.shape[0]
-    rows = pl.ds(pl.multiple_of(lax.axis_index("tp") // CORES * keep, keep), keep)
+    rows = jnp.concatenate([mine_ref[...], peer_ref[...]], axis=1)
     copies = []
     for j in range(count):
         cols = pl.ds(j * tile, tile)
-        sums = sums_ref.at[j % 2]
-        sums[...] = jnp.dot(mine_ref[...], own_ref[:, cols], preferred_element_type=F32) + jnp.dot(
-            peer_ref[...], far_ref[:, cols], preferred_element_type=F32
-        )
-        slots_ref[j] = sums[...].astype(BF16)
-        kept_ref[:, cols] = sums[rows, :]
+        weights = jnp.concatenate([own_ref[:, cols], far_ref[:, cols]], axis=0)
+        slots_ref[j] = jnp.dot(rows, weights, preferred_element_type=F32).astype(BF16)
         copies.append(pltpu.make_async_copy(slots_ref.at[j], out_ref.at[:, cols], sems.at[j]))
         copies[j].start()
     for copy in copies:
         copy.wait()
 
 
-def total_kernel(pieces_ref, kept_ref, out_ref):
-    chip = lax.axis_index("tp") // CORES
+def total_kernel(pieces_ref, out_ref):
     tile = out_ref.shape[1]
     cols = pl.ds(pl.multiple_of(pl.program_id(0) * tile, tile), tile)
-    total = kept_ref[:, cols]
-    for x in range(pieces_ref.shape[0]):
-        total = total + jnp.where(chip == x, 0.0, pieces_ref[x, :, cols].astype(F32))
+    total = pieces_ref[0, :, cols].astype(F32)
+    for x in range(1, pieces_ref.shape[0]):
+        total = total + pieces_ref[x, :, cols].astype(F32)
     out_ref[...] = total.astype(BF16)
 
 
@@ -353,14 +347,13 @@
     chip_groups = [[x * CORES + c for x in range(chips)] for c in range(CORES)]
     keep = half // chips
     tile = min(512, width)
-    sent, kept = pl.pallas_call(
+    sent = pl.pallas_call(
         project_kernel,
         name="project",
         in_specs=[vmem()] * 4,
-        out_specs=[pl.BlockSpec(memory_space=pl.ANY), vmem()],
-        out_shape=[jax.ShapeDtypeStruct((half, width), BF16), jax.ShapeDtypeStruct((keep, width), F32)],
+        out_specs=anywhere,
+        out_shape=jax.ShapeDtypeStruct((half, width), BF16),
         scratch_shapes=[
-            pltpu.VMEM((2, half, tile), F32),
             pltpu.VMEM((width // tile, half, tile), BF16),
             pltpu.SemaphoreType.DMA((width // tile,)),
         ],
@@ -374,12 +367,12 @@
         total_kernel,
         name="total",
         grid=(width // tile,),
-        in_specs=[vmem(), vmem()],
+        in_specs=[vmem()],
         out_specs=pl.BlockSpec((keep, tile), lambda j: (0, j)),
         out_shape=jax.ShapeDtypeStruct((keep, width), BF16),
         compiler_params=limit(16),
         cost_estimate=cost(chips * keep * width, 2 * chips * keep * width),
-    )(pieces.reshape(chips, keep, width), kept)
+    )(pieces.reshape(chips, keep, width))
 
 
 def solution(mesh):

time: 93.4 us -> 93.2 us (level)
  no operation moved by 1% of the time
where the time goes in v5:
time: 93.2 us; the launch traced here: 92.7 us
  blocking collectives  37.7 us (40%)
  starting transfers between devices  27.2 us (29%)
  Pallas kernels  21 us (23%)
  waiting for transfers between devices  6.69 us (7%)
    all_to_all x1, blocking collectives, per_device(): lax.all_to_all(sent, 'tp', 0, 0, axis_index_groups=chip_groups, tiled=True)  29.3 us
    all_to_all x1, starting transfers between devices, per_device(): lax.all_to_all(send, 'ctx', 0, 0, axis_index_groups=row_groups, tiled=True)  15.8 us
    all_to_all x1, blocking collectives, per_device(): lax.all_to_all(shares, 'ctx', 0, 0, axis_index_groups=column_groups, tile...  8.46 us
    ppermute x1, starting transfers between devices, per_device(): far_proj = lax.ppermute(out_proj, 'tp', pairs)  8.08 us
    pallas_call x1, Pallas kernels, per_device(): pl.pallas_call(local_kernel, name='local', grid=(tiles,), in_specs=[smem(...  7.58 us
    all_to_all x1, waiting for transfers between devices, per_device(): lax.all_to_all(send, 'ctx', 0, 0, axis_index_groups=row_groups, tiled=True)  5.55 us
    pallas_call x1, Pallas kernels, per_device(): pl.pallas_call(state_kernel, name='state', in_specs=[smem(), anywhere, an...  4.52 us
    pallas_call x1, Pallas kernels, per_device(): pl.pallas_call(project_kernel, name='project', in_specs=[vmem()] * 4, out...  3.76 us
  transfers between devices with their start and end apart: 3, of which 2 were waited for; matrix products, arithmetic and copies ran while one was open for 0% of the time, Pallas kernels for 13%

profile of v5, /device:TPU:1, one launch (start us, length us, event | category | flops | bytes accessed | tf_op | source)
XLA Modules:
  0.0 92.7 jit_solution(12787347912749297127)
XLA Ops:
  0.0 4.5 %state.1 = (f32[4,512,128]{2,1,0:T(8,128)S(1)}, f32[4,128,128]{2,1,0:T(8,128)S(1)}, bf16[16,16,512]{2,1,0:T(8,128)(2,1)}) custom-call(s32[32]{0:T(128)} %lengths_ref.3, bf16[512,512]{1,0:T(8,128)(2,1)} %gate_hbm.2, bf16[512,512]{1,0:T(8,128)(2,1)} %signal_hbm.1, f32[16,512]{1,0:T(8,128)} %rates_ref.3), custom_call_target="tpu_custom_call" | custom-call | flops 16777216 | bytes 3145728 | tf_op jit(solution)/shard_map/state/pallas_call | solution.py:266
  4.5 15.8 %all-to-all-start = ((bf16[16,16,512]{2,1,0:T(8,128)(2,1)}), bf16[16,16,512]{2,1,0:T(8,128)(2,1)S(1)}, u32[]{:S(2)}, u32[]{:S(2)}) async-start(bf16[16,16,512]{2,1,0:T(8,128)(2,1)} %get-tuple-element.21), calls=%async_computation | async-start | bytes 524288 | tf_op jit(solution)/shard_map/all_to_all | solution.py:291
  20.3 7.6 %local.1 = (f32[4,512,128]{2,1,0:T(8,128)S(1)}, s32[5]{0:T(128)S(1)}, f32[16,512]{1,0:T(8,128)S(1)}, f32[4,128,128]{2,1,0:T(8,128)S(1)}) custom-call(s32[32]{0:T(128)} %lengths_ref.3, f32[4,512,128]{2,1,0:T(8,128)S(1)} %get-tuple-element.18.feed_ref, f32[4,128,128]{2,1,0:T(8,128)S(1)} %get-tuple-element.19.enter_ref, f32[16,512]{1,0:T(8,128)} %rates_ref.3, ...), custom_call_target="tpu_custom_call" | custom-call | flops 33554432 | bytes 2097152 | tf_op jit(solution)/shard_map/local/pallas_call | solution.py:293
  27.9 5.5 %all-to-all-done.states_ref = bf16[16,16,512]{2,1,0:T(8,128)(2,1)S(1)} async-done(((bf16[16,16,512]{2,1,0:T(8,128)(2,1)}), bf16[16,16,512]{2,1,0:T(8,128)(2,1)S(1)}, u32[]{:S(2)}, u32[]{:S(2)}) %all-to-all-start) | async-done | bytes 262176 | tf_op jit(solution)/shard_map/all_to_all | solution.py:291
  33.4 8.1 %collective-permute-start.1 = (bf16[512,4096]{1,0:T(8,128)(2,1)}, bf16[512,4096]{1,0:T(8,128)(2,1)S(1)}, u32[]{:S(2)}, u32[]{:S(2)}) collective-permute-start(bf16[512,4096]{1,0:T(8,128)(2,1)} %proj_hbm), channel_id=1, source_target_pairs={{0,1},{1,0},{2,3},{3,2},{4,5},{5,4},{6,7},{7,6},{8,9},{9,8},{10,11... | collective-permute-start | bytes 12582920 | tf_op jit(solution)/shard_map/ppermute | solution.py:311
  41.5 1.2 %relay.1 = bf16[4,16,512]{2,1,0:T(8,128)(2,1)S(1)} custom-call(s32[5]{0:T(128)S(1)} %get-tuple-element.20.info_ref, bf16[16,16,512]{2,1,0:T(8,128)(2,1)S(1)} %all-to-all-done.states_ref, f32[16,512]{1,0:T(8,128)} %rates_ref.3), custom_call_target="tpu_custom_call" | custom-call | flops 2097152 | bytes 327680 | tf_op jit(solution)/shard_map/relay/pallas_call | solution.py:314
  42.7 8.5 %all_to_all.19.shares_ref = bf16[4,16,512]{2,1,0:T(8,128)(2,1)S(1)} all-to-all(bf16[4,16,512]{2,1,0:T(8,128)(2,1)S(1)} %relay.1), channel_id=1, replica_groups={{0,128,256,384},{8,136,264,392},{16,144,272,400},{24,152,280,408},{32,1..., dimensions={0} | all-to-all | bytes 131072 | tf_op jit(solution)/shard_map/all_to_all | solution.py:325
  51.2 3.0 %hidden.1 = (bf16[256,512]{1,0:T(8,128)(2,1)S(1)}, bf16[256,512]{1,0:T(8,128)(2,1)S(1)}, bf16[512,4096]{1,0:T(8,128)(2,1)S(1)}) custom-call(s32[5]{0:T(128)S(1)} %get-tuple-element.20.info_ref, bf16[4,16,512]{2,1,0:T(8,128)(2,1)S(1)} %all_to_all.19.shares_ref, f32[16,512]{1,0:T(8,128)S(1)} %get-tuple-element.24.decay_ref, ...), custom_call_target="tpu_custom_call" | custom-call | flops 12582912 | bytes 2097152 | tf_op jit(solution)/shard_map/hidden/pallas_call | solution.py:327
  54.2 3.4 %collective-permute-start = (bf16[256,512]{1,0:T(8,128)(2,1)S(1)}, bf16[256,512]{1,0:T(8,128)(2,1)S(1)}, u32[]{:S(2)}, u32[]{:S(2)}) collective-permute-start(bf16[256,512]{1,0:T(8,128)(2,1)S(1)} %get-tuple-element.29), channel_id=1, source_target_pairs={{0,1},{1,0},{2,3},{3,2},{4,5},{5,4},{6,7},{7,6},{8,9},{9,8},{10,11... | collective-permute-start | bytes 786440 | tf_op jit(solution)/shard_map/ppermute | solution.py:345
  57.5 1.1 %collective-permute-done.peer_ref = bf16[256,512]{1,0:T(8,128)(2,1)S(1)} collective-permute-done((bf16[256,512]{1,0:T(8,128)(2,1)S(1)}, bf16[256,512]{1,0:T(8,128)(2,1)S(1)}, u32[]{:S(2)}, u32[]{:S(2)}) %collective-permute-start) | collective-permute-done | bytes 262176 | tf_op jit(solution)/shard_map/ppermute | solution.py:345
  58.7 0.0 collective-permute-done.1.far_ref
  58.7 3.8 %project.1 = bf16[256,4096]{1,0:T(8,128)(2,1)S(1)} custom-call(bf16[256,512]{1,0:T(8,128)(2,1)S(1)} %get-tuple-element.28.mine_ref, bf16[256,512]{1,0:T(8,128)(2,1)S(1)} %collective-permute-done.peer_ref, bf16[512,4096]{1,0:T(8,128)(2,1)S(1)} %get-tuple-element.30.own_ref, bf16[512,4096]{1,0:T(8,128)(2,1)S(1)} %collective-permute-done.1.far_ref), custom_call_target="tpu_custom_call" | custom-call | flops 2147483648 | bytes 8388608 | tf_op jit(solution)/shard_map/project/pallas_call | solution.py:350
  62.5 29.3 %all_to_all.20.pieces_ref = bf16[4,64,4096]{2,1,0:T(8,128)(2,1)S(1)} all-to-all(bf16[4,64,4096]{2,1,0:T(8,128)(2,1)S(1)} %bitcast.2), channel_id=1, replica_groups={{0,2,4,6},{1,3,5,7},{8,10,12,14},{9,11,13,15},{16,18,20,22},{17,19,21,2..., dimensions={0} | all-to-all | bytes 4194304 | tf_op jit(solution)/shard_map/all_to_all | solution.py:363
  91.7 1.0 %total.1 = bf16[64,4096]{1,0:T(8,128)(2,1)} custom-call(bf16[4,64,4096]{2,1,0:T(8,128)(2,1)S(1)} %all_to_all.20.pieces_ref), custom_call_target="tpu_custom_call" | custom-call | flops 1048576 | bytes 2097152 | tf_op jit(solution)/shard_map/total/pallas_call | solution.py:366
Async XLA Ops:
  4.5 28.9 %all-to-all-start = ((bf16[16,16,512]{2,1,0:T(8,128)(2,1)}), bf16[16,16,512]{2,1,0:T(8,128)(2,1)S(1)}, u32[]{:S(2)}, u32[]{:S(2)}) async-start(bf16[16,16,512]{2,1,0:T(8,128)(2,1)} %get-tuple-element.21), calls=%async_computation | async-start | bytes 524288 | tf_op jit(solution)/shard_map/all_to_all | solution.py:291
  33.4 25.3 %collective-permute-start.1 = (bf16[512,4096]{1,0:T(8,128)(2,1)}, bf16[512,4096]{1,0:T(8,128)(2,1)S(1)}, u32[]{:S(2)}, u32[]{:S(2)}) collective-permute-start(bf16[512,4096]{1,0:T(8,128)(2,1)} %proj_hbm), channel_id=1, source_target_pairs={{0,1},{1,0},{2,3},{3,2},{4,5},{5,4},{6,7},{7,6},{8,9},{9,8},{10,11... | collective-permute-start | bytes 12582920 | tf_op jit(solution)/shard_map/ppermute | solution.py:311
  54.2 4.5 %collective-permute-start = (bf16[256,512]{1,0:T(8,128)(2,1)S(1)}, bf16[256,512]{1,0:T(8,128)(2,1)S(1)}, u32[]{:S(2)}, u32[]{:S(2)}) collective-permute-start(bf16[256,512]{1,0:T(8,128)(2,1)S(1)} %get-tuple-element.29), channel_id=1, source_target_pairs={{0,1},{1,0},{2,3},{3,2},{4,5},{5,4},{6,7},{7,6},{8,9},{9,8},{10,11... | collective-permute-start | bytes 786440 | tf_op jit(solution)/shard_map/ppermute | solution.py:345

commit v6 on v5

--- a/solution.py
+++ b/solution.py
@@ -216,14 +216,20 @@
         move.wait()
 
 
-def project_kernel(mine_ref, peer_ref, own_ref, far_ref, out_ref, slots_ref, sems):
+def own_kernel(mine_ref, own_ref, out_ref):
+    tile = 512
+    for j in range(0, out_ref.shape[1], tile):
+        cols = slice(j, j + tile)
+        out_ref[:, cols] = jnp.dot(mine_ref[...], own_ref[:, cols], preferred_element_type=F32)
+
+
+def project_kernel(peer_ref, far_ref, part_ref, out_ref, slots_ref, sems):
     count, _, tile = slots_ref.shape
-    rows = jnp.concatenate([mine_ref[...], peer_ref[...]], axis=1)
     copies = []
     for j in range(count):
         cols = pl.ds(j * tile, tile)
-        weights = jnp.concatenate([own_ref[:, cols], far_ref[:, cols]], axis=0)
-        slots_ref[j] = jnp.dot(rows, weights, preferred_element_type=F32).astype(BF16)
+        far = jnp.dot(peer_ref[...], far_ref[:, cols], preferred_element_type=F32)
+        slots_ref[j] = (part_ref[:, cols] + far).astype(BF16)
         copies.append(pltpu.make_async_copy(slots_ref.at[j], out_ref.at[:, cols], sems.at[j]))
         copies[j].start()
     for copy in copies:
@@ -347,10 +353,19 @@
     chip_groups = [[x * CORES + c for x in range(chips)] for c in range(CORES)]
     keep = half // chips
     tile = min(512, width)
+    part = pl.pallas_call(
+        own_kernel,
+        name="own",
+        in_specs=[vmem()] * 2,
+        out_specs=vmem(),
+        out_shape=jax.ShapeDtypeStruct((half, width), F32),
+        compiler_params=limit(8),
+        cost_estimate=cost(2 * half * channels * width, 2 * channels * width),
+    )(mine, weights)
     sent = pl.pallas_call(
         project_kernel,
         name="project",
-        in_specs=[vmem()] * 4,
+        in_specs=[vmem()] * 3,
         out_specs=anywhere,
         out_shape=jax.ShapeDtypeStruct((half, width), BF16),
         scratch_shapes=[
@@ -358,8 +373,8 @@
             pltpu.SemaphoreType.DMA((width // tile,)),
         ],
         compiler_params=limit(16),
-        cost_estimate=cost(4 * half * channels * width, 4 * channels * width),
-    )(mine, peer, weights, far_proj)
+        cost_estimate=cost(2 * half * channels * width, 2 * channels * width),
+    )(peer, far_proj, part)
     pieces = lax.all_to_all(sent, "tp", 0, 0, axis_index_groups=chip_groups, tiled=True)
 
     tile = min(2048, width)

time: 93.2 us -> 92.6 us (level)
  waiting for transfers between devices: 6.69 us -> 5.54 us
    ppermute x1, waiting for transfers between devices: 1.14 us -> 0.01 us  [per_device(): peer = lax.ppermute(other, 'tp', pairs)]
    pallas_call x1 -> x2, Pallas kernels: 3.76 us -> 3.89 us  [the longest x1 2.64 us: per_device(): pl.pallas_call(project_kernel, name='project', in_specs=[vmem()] * 3, out...]
  transfers between devices with their start and end apart: 3 -> 3, of which waited for: 2 -> 1; matrix products, arithmetic and copies ran while one was open for 0% -> 0% of each run, Pallas kernels for 13% -> 14%
where the time goes in v6:
time: 92.6 us; the launch traced here: 92.2 us
  blocking collectives  38.2 us (41%)
  starting transfers between devices  27.2 us (29%)
  Pallas kernels  21.2 us (23%)
  waiting for transfers between devices  5.54 us (6%)
    all_to_all x1, blocking collectives, per_device(): lax.all_to_all(sent, 'tp', 0, 0, axis_index_groups=chip_groups, tiled=True)  29.7 us
    all_to_all x1, starting transfers between devices, per_device(): lax.all_to_all(send, 'ctx', 0, 0, axis_index_groups=row_groups, tiled=True)  15.8 us
    all_to_all x1, blocking collectives, per_device(): lax.all_to_all(shares, 'ctx', 0, 0, axis_index_groups=column_groups, tile...  8.46 us
    ppermute x1, starting transfers between devices, per_device(): far_proj = lax.ppermute(out_proj, 'tp', pairs)  8.08 us
    pallas_call x1, Pallas kernels, per_device(): pl.pallas_call(local_kernel, name='local', grid=(tiles,), in_specs=[smem(...  7.59 us
    all_to_all x1, waiting for transfers between devices, per_device(): lax.all_to_all(send, 'ctx', 0, 0, axis_index_groups=row_groups, tiled=True)  5.54 us
    pallas_call x1, Pallas kernels, per_device(): pl.pallas_call(state_kernel, name='state', in_specs=[smem(), anywhere, an...  4.52 us
    ppermute x1, starting transfers between devices, per_device(): peer = lax.ppermute(other, 'tp', pairs)  3.35 us
  transfers between devices with their start and end apart: 3, of which 1 were waited for; matrix products, arithmetic and copies ran while one was open for 0% of the time, Pallas kernels for 14%

profile of v6, /device:TPU:1, one launch (start us, length us, event | category | flops | bytes accessed | tf_op | source)
XLA Modules:
  0.0 92.2 jit_solution(10660341805424714885)
XLA Ops:
  0.0 4.5 %state.1 = (f32[4,512,128]{2,1,0:T(8,128)S(1)}, f32[4,128,128]{2,1,0:T(8,128)S(1)}, bf16[16,16,512]{2,1,0:T(8,128)(2,1)}) custom-call(s32[32]{0:T(128)} %lengths_ref.3, bf16[512,512]{1,0:T(8,128)(2,1)} %gate_hbm.2, bf16[512,512]{1,0:T(8,128)(2,1)} %signal_hbm.1, f32[16,512]{1,0:T(8,128)} %rates_ref.3), custom_call_target="tpu_custom_call" | custom-call | flops 16777216 | bytes 3145728 | tf_op jit(solution)/shard_map/state/pallas_call | solution.py:272
  4.5 15.8 %all-to-all-start = ((bf16[16,16,512]{2,1,0:T(8,128)(2,1)}), bf16[16,16,512]{2,1,0:T(8,128)(2,1)S(1)}, u32[]{:S(2)}, u32[]{:S(2)}) async-start(bf16[16,16,512]{2,1,0:T(8,128)(2,1)} %get-tuple-element.21), calls=%async_computation | async-start | bytes 524288 | tf_op jit(solution)/shard_map/all_to_all | solution.py:297
  20.3 7.6 %local.1 = (f32[4,512,128]{2,1,0:T(8,128)S(1)}, s32[5]{0:T(128)S(1)}, f32[16,512]{1,0:T(8,128)S(1)}, f32[4,128,128]{2,1,0:T(8,128)S(1)}) custom-call(s32[32]{0:T(128)} %lengths_ref.3, f32[4,512,128]{2,1,0:T(8,128)S(1)} %get-tuple-element.18.feed_ref, f32[4,128,128]{2,1,0:T(8,128)S(1)} %get-tuple-element.19.enter_ref, f32[16,512]{1,0:T(8,128)} %rates_ref.3, ...), custom_call_target="tpu_custom_call" | custom-call | flops 33554432 | bytes 2097152 | tf_op jit(solution)/shard_map/local/pallas_call | solution.py:299
  27.9 5.5 %all-to-all-done.states_ref = bf16[16,16,512]{2,1,0:T(8,128)(2,1)S(1)} async-done(((bf16[16,16,512]{2,1,0:T(8,128)(2,1)}), bf16[16,16,512]{2,1,0:T(8,128)(2,1)S(1)}, u32[]{:S(2)}, u32[]{:S(2)}) %all-to-all-start) | async-done | bytes 262176 | tf_op jit(solution)/shard_map/all_to_all | solution.py:297
  33.4 8.1 %collective-permute-start.1 = (bf16[512,4096]{1,0:T(8,128)(2,1)}, bf16[512,4096]{1,0:T(8,128)(2,1)S(1)}, u32[]{:S(2)}, u32[]{:S(2)}) collective-permute-start(bf16[512,4096]{1,0:T(8,128)(2,1)} %proj_hbm), channel_id=1, source_target_pairs={{0,1},{1,0},{2,3},{3,2},{4,5},{5,4},{6,7},{7,6},{8,9},{9,8},{10,11... | collective-permute-start | bytes 12582920 | tf_op jit(solution)/shard_map/ppermute | solution.py:317
  41.5 1.2 %relay.1 = bf16[4,16,512]{2,1,0:T(8,128)(2,1)S(1)} custom-call(s32[5]{0:T(128)S(1)} %get-tuple-element.20.info_ref, bf16[16,16,512]{2,1,0:T(8,128)(2,1)S(1)} %all-to-all-done.states_ref, f32[16,512]{1,0:T(8,128)} %rates_ref.3), custom_call_target="tpu_custom_call" | custom-call | flops 2097152 | bytes 327680 | tf_op jit(solution)/shard_map/relay/pallas_call | solution.py:320
  42.7 8.5 %all_to_all.19.shares_ref = bf16[4,16,512]{2,1,0:T(8,128)(2,1)S(1)} all-to-all(bf16[4,16,512]{2,1,0:T(8,128)(2,1)S(1)} %relay.1), channel_id=1, replica_groups={{0,128,256,384},{8,136,264,392},{16,144,272,400},{24,152,280,408},{32,1..., dimensions={0} | all-to-all | bytes 131072 | tf_op jit(solution)/shard_map/all_to_all | solution.py:331
  51.2 3.0 %hidden.1 = (bf16[256,512]{1,0:T(8,128)(2,1)S(1)}, bf16[256,512]{1,0:T(8,128)(2,1)S(1)}, bf16[512,4096]{1,0:T(8,128)(2,1)S(1)}) custom-call(s32[5]{0:T(128)S(1)} %get-tuple-element.20.info_ref, bf16[4,16,512]{2,1,0:T(8,128)(2,1)S(1)} %all_to_all.19.shares_ref, f32[16,512]{1,0:T(8,128)S(1)} %get-tuple-element.24.decay_ref, ...), custom_call_target="tpu_custom_call" | custom-call | flops 12582912 | bytes 2097152 | tf_op jit(solution)/shard_map/hidden/pallas_call | solution.py:333
  54.2 3.4 %collective-permute-start = (bf16[256,512]{1,0:T(8,128)(2,1)S(1)}, bf16[256,512]{1,0:T(8,128)(2,1)S(1)}, u32[]{:S(2)}, u32[]{:S(2)}) collective-permute-start(bf16[256,512]{1,0:T(8,128)(2,1)S(1)} %get-tuple-element.28), channel_id=1, source_target_pairs={{0,1},{1,0},{2,3},{3,2},{4,5},{5,4},{6,7},{7,6},{8,9},{9,8},{10,11... | collective-permute-start | bytes 786440 | tf_op jit(solution)/shard_map/ppermute | solution.py:351
  57.5 1.3 %own.1.part_ref = f32[256,4096]{1,0:T(8,128)S(1)} custom-call(bf16[256,512]{1,0:T(8,128)(2,1)S(1)} %get-tuple-element.29.mine_ref, bf16[512,4096]{1,0:T(8,128)(2,1)S(1)} %get-tuple-element.30.own_ref), custom_call_target="tpu_custom_call" | custom-call | flops 1073741824 | bytes 4194304 | tf_op jit(solution)/shard_map/own/pallas_call | solution.py:356
  58.8 0.0 collective-permute-done.peer_ref
  58.8 0.0 collective-permute-done.1.far_ref
  58.8 2.6 %project.1 = bf16[256,4096]{1,0:T(8,128)(2,1)S(1)} custom-call(bf16[256,512]{1,0:T(8,128)(2,1)S(1)} %collective-permute-done.peer_ref, bf16[512,4096]{1,0:T(8,128)(2,1)S(1)} %collective-permute-done.1.far_ref, f32[256,4096]{1,0:T(8,128)S(1)} %own.1.part_ref), custom_call_target="tpu_custom_call" | custom-call | flops 1073741824 | bytes 4194304 | tf_op jit(solution)/shard_map/project/pallas_call | solution.py:365
  61.5 29.7 %all_to_all.20.pieces_ref = bf16[4,64,4096]{2,1,0:T(8,128)(2,1)S(1)} all-to-all(bf16[4,64,4096]{2,1,0:T(8,128)(2,1)S(1)} %bitcast.2), channel_id=1, replica_groups={{0,2,4,6},{1,3,5,7},{8,10,12,14},{9,11,13,15},{16,18,20,22},{17,19,21,2..., dimensions={0} | all-to-all | bytes 4194304 | tf_op jit(solution)/shard_map/all_to_all | solution.py:378
  91.2 1.0 %total.1 = bf16[64,4096]{1,0:T(8,128)(2,1)} custom-call(bf16[4,64,4096]{2,1,0:T(8,128)(2,1)S(1)} %all_to_all.20.pieces_ref), custom_call_target="tpu_custom_call" | custom-call | flops 1048576 | bytes 2097152 | tf_op jit(solution)/shard_map/total/pallas_call | solution.py:381
Async XLA Ops:
  4.5 28.9 %all-to-all-start = ((bf16[16,16,512]{2,1,0:T(8,128)(2,1)}), bf16[16,16,512]{2,1,0:T(8,128)(2,1)S(1)}, u32[]{:S(2)}, u32[]{:S(2)}) async-start(bf16[16,16,512]{2,1,0:T(8,128)(2,1)} %get-tuple-element.21), calls=%async_computation | async-start | bytes 524288 | tf_op jit(solution)/shard_map/all_to_all | solution.py:297
  33.4 25.4 %collective-permute-start.1 = (bf16[512,4096]{1,0:T(8,128)(2,1)}, bf16[512,4096]{1,0:T(8,128)(2,1)S(1)}, u32[]{:S(2)}, u32[]{:S(2)}) collective-permute-start(bf16[512,4096]{1,0:T(8,128)(2,1)} %proj_hbm), channel_id=1, source_target_pairs={{0,1},{1,0},{2,3},{3,2},{4,5},{5,4},{6,7},{7,6},{8,9},{9,8},{10,11... | collective-permute-start | bytes 12582920 | tf_op jit(solution)/shard_map/ppermute | solution.py:317
  54.2 4.6 %collective-permute-start = (bf16[256,512]{1,0:T(8,128)(2,1)S(1)}, bf16[256,512]{1,0:T(8,128)(2,1)S(1)}, u32[]{:S(2)}, u32[]{:S(2)}) collective-permute-start(bf16[256,512]{1,0:T(8,128)(2,1)S(1)} %get-tuple-element.28), channel_id=1, source_target_pairs={{0,1},{1,0},{2,3},{3,2},{4,5},{5,4},{6,7},{7,6},{8,9},{9,8},{10,11... | collective-permute-start | bytes 786440 | tf_op jit(solution)/shard_map/ppermute | solution.py:351

commit v7 on v6

--- a/solution.py
+++ b/solution.py
@@ -223,17 +223,12 @@
         out_ref[:, cols] = jnp.dot(mine_ref[...], own_ref[:, cols], preferred_element_type=F32)
 
 
-def project_kernel(peer_ref, far_ref, part_ref, out_ref, slots_ref, sems):
-    count, _, tile = slots_ref.shape
-    copies = []
-    for j in range(count):
-        cols = pl.ds(j * tile, tile)
+def project_kernel(peer_ref, far_ref, part_ref, out_ref):
+    tile = 512
+    for j in range(0, out_ref.shape[1], tile):
+        cols = slice(j, j + tile)
         far = jnp.dot(peer_ref[...], far_ref[:, cols], preferred_element_type=F32)
-        slots_ref[j] = (part_ref[:, cols] + far).astype(BF16)
-        copies.append(pltpu.make_async_copy(slots_ref.at[j], out_ref.at[:, cols], sems.at[j]))
-        copies[j].start()
-    for copy in copies:
-        copy.wait()
+        out_ref[:, cols] = (part_ref[:, cols] + far).astype(BF16)
 
 
 def total_kernel(pieces_ref, out_ref):
@@ -366,12 +361,8 @@
         project_kernel,
         name="project",
         in_specs=[vmem()] * 3,
-        out_specs=anywhere,
+        out_specs=vmem(),
         out_shape=jax.ShapeDtypeStruct((half, width), BF16),
-        scratch_shapes=[
-            pltpu.VMEM((width // tile, half, tile), BF16),
-            pltpu.SemaphoreType.DMA((width // tile,)),
-        ],
         compiler_params=limit(16),
         cost_estimate=cost(2 * half * channels * width, 2 * channels * width),
     )(peer, far_proj, part)

time: 92.6 us -> 91.3 us (0.986)
  Pallas kernels: 21.2 us -> 19.9 us
    pallas_call x1, Pallas kernels: 2.64 us -> 1.35 us  [per_device(): pl.pallas_call(project_kernel, name='project', in_specs=[vmem()] * 3, out...]
where the time goes in v7:
time: 91.3 us; the launch traced here: 90.9 us
  blocking collectives  38.2 us (42%)
  starting transfers between devices  27.2 us (30%)
  Pallas kernels  19.9 us (22%)
  waiting for transfers between devices  5.55 us (6%)
    all_to_all x1, blocking collectives, per_device(): lax.all_to_all(sent, 'tp', 0, 0, axis_index_groups=chip_groups, tiled=True)  29.7 us
    all_to_all x1, starting transfers between devices, per_device(): lax.all_to_all(send, 'ctx', 0, 0, axis_index_groups=row_groups, tiled=True)  15.8 us
    all_to_all x1, blocking collectives, per_device(): lax.all_to_all(shares, 'ctx', 0, 0, axis_index_groups=column_groups, tile...  8.46 us
    ppermute x1, starting transfers between devices, per_device(): far_proj = lax.ppermute(out_proj, 'tp', pairs)  8.08 us
    pallas_call x1, Pallas kernels, per_device(): pl.pallas_call(local_kernel, name='local', grid=(tiles,), in_specs=[smem(...  7.58 us
    all_to_all x1, waiting for transfers between devices, per_device(): lax.all_to_all(send, 'ctx', 0, 0, axis_index_groups=row_groups, tiled=True)  5.55 us
    pallas_call x1, Pallas kernels, per_device(): pl.pallas_call(state_kernel, name='state', in_specs=[smem(), anywhere, an...  4.52 us
    ppermute x1, starting transfers between devices, per_device(): peer = lax.ppermute(other, 'tp', pairs)  3.35 us
  transfers between devices with their start and end apart: 3, of which 1 were waited for; matrix products, arithmetic and copies ran while one was open for 0% of the time, Pallas kernels for 14%

profile of v7, /device:TPU:1, one launch (start us, length us, event | category | flops | bytes accessed | tf_op | source)
XLA Modules:
  0.0 90.9 jit_solution(4407038815323745180)
XLA Ops:
  0.0 4.5 %state.1 = (f32[4,512,128]{2,1,0:T(8,128)S(1)}, f32[4,128,128]{2,1,0:T(8,128)S(1)}, bf16[16,16,512]{2,1,0:T(8,128)(2,1)}) custom-call(s32[32]{0:T(128)} %lengths_ref.3, bf16[512,512]{1,0:T(8,128)(2,1)} %gate_hbm.2, bf16[512,512]{1,0:T(8,128)(2,1)} %signal_hbm.1, f32[16,512]{1,0:T(8,128)} %rates_ref.3), custom_call_target="tpu_custom_call" | custom-call | flops 16777216 | bytes 3145728 | tf_op jit(solution)/shard_map/state/pallas_call | solution.py:267
  4.5 15.8 %all-to-all-start = ((bf16[16,16,512]{2,1,0:T(8,128)(2,1)}), bf16[16,16,512]{2,1,0:T(8,128)(2,1)S(1)}, u32[]{:S(2)}, u32[]{:S(2)}) async-start(bf16[16,16,512]{2,1,0:T(8,128)(2,1)} %get-tuple-element.21), calls=%async_computation | async-start | bytes 524288 | tf_op jit(solution)/shard_map/all_to_all | solution.py:292
  20.3 7.6 %local.1 = (f32[4,512,128]{2,1,0:T(8,128)S(1)}, s32[5]{0:T(128)S(1)}, f32[16,512]{1,0:T(8,128)S(1)}, f32[4,128,128]{2,1,0:T(8,128)S(1)}) custom-call(s32[32]{0:T(128)} %lengths_ref.3, f32[4,512,128]{2,1,0:T(8,128)S(1)} %get-tuple-element.18.feed_ref, f32[4,128,128]{2,1,0:T(8,128)S(1)} %get-tuple-element.19.enter_ref, f32[16,512]{1,0:T(8,128)} %rates_ref.3, ...), custom_call_target="tpu_custom_call" | custom-call | flops 33554432 | bytes 2097152 | tf_op jit(solution)/shard_map/local/pallas_call | solution.py:294
  27.9 5.5 %all-to-all-done.states_ref = bf16[16,16,512]{2,1,0:T(8,128)(2,1)S(1)} async-done(((bf16[16,16,512]{2,1,0:T(8,128)(2,1)}), bf16[16,16,512]{2,1,0:T(8,128)(2,1)S(1)}, u32[]{:S(2)}, u32[]{:S(2)}) %all-to-all-start) | async-done | bytes 262176 | tf_op jit(solution)/shard_map/all_to_all | solution.py:292
  33.4 8.1 %collective-permute-start.1 = (bf16[512,4096]{1,0:T(8,128)(2,1)}, bf16[512,4096]{1,0:T(8,128)(2,1)S(1)}, u32[]{:S(2)}, u32[]{:S(2)}) collective-permute-start(bf16[512,4096]{1,0:T(8,128)(2,1)} %proj_hbm), channel_id=1, source_target_pairs={{0,1},{1,0},{2,3},{3,2},{4,5},{5,4},{6,7},{7,6},{8,9},{9,8},{10,11... | collective-permute-start | bytes 12582920 | tf_op jit(solution)/shard_map/ppermute | solution.py:312
  41.5 1.2 %relay.1 = bf16[4,16,512]{2,1,0:T(8,128)(2,1)S(1)} custom-call(s32[5]{0:T(128)S(1)} %get-tuple-element.20.info_ref, bf16[16,16,512]{2,1,0:T(8,128)(2,1)S(1)} %all-to-all-done.states_ref, f32[16,512]{1,0:T(8,128)} %rates_ref.3), custom_call_target="tpu_custom_call" | custom-call | flops 2097152 | bytes 327680 | tf_op jit(solution)/shard_map/relay/pallas_call | solution.py:315
  42.7 8.5 %all_to_all.19.shares_ref = bf16[4,16,512]{2,1,0:T(8,128)(2,1)S(1)} all-to-all(bf16[4,16,512]{2,1,0:T(8,128)(2,1)S(1)} %relay.1), channel_id=1, replica_groups={{0,128,256,384},{8,136,264,392},{16,144,272,400},{24,152,280,408},{32,1..., dimensions={0} | all-to-all | bytes 131072 | tf_op jit(solution)/shard_map/all_to_all | solution.py:326
  51.2 3.0 %hidden.1 = (bf16[256,512]{1,0:T(8,128)(2,1)S(1)}, bf16[256,512]{1,0:T(8,128)(2,1)S(1)}, bf16[512,4096]{1,0:T(8,128)(2,1)S(1)}) custom-call(s32[5]{0:T(128)S(1)} %get-tuple-element.20.info_ref, bf16[4,16,512]{2,1,0:T(8,128)(2,1)S(1)} %all_to_all.19.shares_ref, f32[16,512]{1,0:T(8,128)S(1)} %get-tuple-element.24.decay_ref, ...), custom_call_target="tpu_custom_call" | custom-call | flops 12582912 | bytes 2097152 | tf_op jit(solution)/shard_map/hidden/pallas_call | solution.py:328
  54.2 3.4 %collective-permute-start = (bf16[256,512]{1,0:T(8,128)(2,1)S(1)}, bf16[256,512]{1,0:T(8,128)(2,1)S(1)}, u32[]{:S(2)}, u32[]{:S(2)}) collective-permute-start(bf16[256,512]{1,0:T(8,128)(2,1)S(1)} %get-tuple-element.28), channel_id=1, source_target_pairs={{0,1},{1,0},{2,3},{3,2},{4,5},{5,4},{6,7},{7,6},{8,9},{9,8},{10,11... | collective-permute-start | bytes 786440 | tf_op jit(solution)/shard_map/ppermute | solution.py:346
  57.5 1.3 %own.1.part_ref = f32[256,4096]{1,0:T(8,128)S(1)} custom-call(bf16[256,512]{1,0:T(8,128)(2,1)S(1)} %get-tuple-element.29.mine_ref, bf16[512,4096]{1,0:T(8,128)(2,1)S(1)} %get-tuple-element.30.own_ref), custom_call_target="tpu_custom_call" | custom-call | flops 1073741824 | bytes 4194304 | tf_op jit(solution)/shard_map/own/pallas_call | solution.py:351
  58.8 0.0 collective-permute-done.peer_ref
  58.8 0.0 collective-permute-done.1.far_ref
  58.8 1.3 %project.1 = bf16[256,4096]{1,0:T(8,128)(2,1)S(1)} custom-call(bf16[256,512]{1,0:T(8,128)(2,1)S(1)} %collective-permute-done.peer_ref, bf16[512,4096]{1,0:T(8,128)(2,1)S(1)} %collective-permute-done.1.far_ref, f32[256,4096]{1,0:T(8,128)S(1)} %own.1.part_ref), custom_call_target="tpu_custom_call" | custom-call | flops 1073741824 | bytes 4194304 | tf_op jit(solution)/shard_map/project/pallas_call | solution.py:360
  60.2 29.7 %all_to_all.20.pieces_ref = bf16[4,64,4096]{2,1,0:T(8,128)(2,1)S(1)} all-to-all(bf16[4,64,4096]{2,1,0:T(8,128)(2,1)S(1)} %bitcast.2), channel_id=1, replica_groups={{0,2,4,6},{1,3,5,7},{8,10,12,14},{9,11,13,15},{16,18,20,22},{17,19,21,2..., dimensions={0} | all-to-all | bytes 4194304 | tf_op jit(solution)/shard_map/all_to_all | solution.py:369
  89.9 1.0 %total.1 = bf16[64,4096]{1,0:T(8,128)(2,1)} custom-call(bf16[4,64,4096]{2,1,0:T(8,128)(2,1)S(1)} %all_to_all.20.pieces_ref), custom_call_target="tpu_custom_call" | custom-call | flops 1048576 | bytes 2097152 | tf_op jit(solution)/shard_map/total/pallas_call | solution.py:372
Async XLA Ops:
  4.5 28.9 %all-to-all-start = ((bf16[16,16,512]{2,1,0:T(8,128)(2,1)}), bf16[16,16,512]{2,1,0:T(8,128)(2,1)S(1)}, u32[]{:S(2)}, u32[]{:S(2)}) async-start(bf16[16,16,512]{2,1,0:T(8,128)(2,1)} %get-tuple-element.21), calls=%async_computation | async-start | bytes 524288 | tf_op jit(solution)/shard_map/all_to_all | solution.py:292
  33.4 25.4 %collective-permute-start.1 = (bf16[512,4096]{1,0:T(8,128)(2,1)}, bf16[512,4096]{1,0:T(8,128)(2,1)S(1)}, u32[]{:S(2)}, u32[]{:S(2)}) collective-permute-start(bf16[512,4096]{1,0:T(8,128)(2,1)} %proj_hbm), channel_id=1, source_target_pairs={{0,1},{1,0},{2,3},{3,2},{4,5},{5,4},{6,7},{7,6},{8,9},{9,8},{10,11... | collective-permute-start | bytes 12582920 | tf_op jit(solution)/shard_map/ppermute | solution.py:312
  54.2 4.6 %collective-permute-start = (bf16[256,512]{1,0:T(8,128)(2,1)S(1)}, bf16[256,512]{1,0:T(8,128)(2,1)S(1)}, u32[]{:S(2)}, u32[]{:S(2)}) collective-permute-start(bf16[256,512]{1,0:T(8,128)(2,1)S(1)} %get-tuple-element.28), channel_id=1, source_target_pairs={{0,1},{1,0},{2,3},{3,2},{4,5},{5,4},{6,7},{7,6},{8,9},{9,8},{10,11... | collective-permute-start | bytes 786440 | tf_op jit(solution)/shard_map/ppermute | solution.py:346
